TPU v7x, 32 devices: a whole 2x2x4 slice. The times are simulated.
32 devices in a mesh: energy: 16 (over z, y, x), slab: 2 (over core).
Axes of the slice: x: 2, y: 2, z: 4, core: 2. Of those that a mesh axis runs over, the one named last changes fastest.
Arguments:
- green0: bfloat16 [16, 2, 2, 384, 384], P('energy', 'slab'), may hold values from -6 to 6
- coupling: bfloat16 [2, 3, 384, 384], P('slab'), may hold values from -0.09375 to 0.09375
Outputs:
- green: bfloat16 [16, 2, 2, 384, 384], P('energy', 'slab')
All inputs are finite; a program needn't handle non-finite values.
Results may differ from a plain program's by a relative error of at most 0.012.
Values may be sent and summed in bfloat16 or wider, within the bound.
No kernel may reach another device: no remote copies, remote signals or barrier semaphores. Data moves between devices by JAX's collectives and lax.ppermute only.
A program may use at most 64 MiB of HBM per device.

v0:
```python
import jax
import jax.numpy as jnp
from jax import lax
from jax.sharding import PartitionSpec as P

OFFSET = 7
ITERS = 2


def passed_along(value, axis, steps):
    count = lax.axis_size(axis)
    first, last = (max(0, -steps), min(count, count - steps))
    return lax.ppermute(value, axis, [(source, source + steps) for source in range(first, last)])


def with_halo(block, sides, width):
    for axis, dim in sides:
        count = lax.axis_size(axis)
        forward = [(i, i + 1) for i in range(count - 1)]
        backward = [(target, source) for source, target in forward]
        low = lax.ppermute(
            lax.slice_in_dim(block, block.shape[dim] - width, None, axis=dim), axis, forward
        )
        high = lax.ppermute(lax.slice_in_dim(block, 0, width, axis=dim), axis, backward)
        block = jnp.concatenate([low, block, high], axis=dim)
    return block


def dyson(green0, coupling, summed):
    count = green0.shape[1]
    size = green0.shape[-1]
    sigma = jnp.zeros(green0.shape, jnp.float32)
    for index in range(3):
        part = summed[:, index : index + count]
        weights = coupling[:, index]
        left = jnp.einsum(
            "sij,escjk->escik", weights, part, preferred_element_type=jnp.float32
        ).astype(jnp.bfloat16)
        sigma = sigma + jnp.einsum(
            "escij,skj->escik", left, weights, preferred_element_type=jnp.float32
        )
    sigma = sigma.astype(jnp.bfloat16)
    green_re = green0[:, :, 0]
    green_im = green0[:, :, 1]
    form = "esij,esjk->esik"
    prod_re = jnp.einsum(
        form, green_re, sigma[:, :, 0], preferred_element_type=jnp.float32
    ) - jnp.einsum(form, green_im, sigma[:, :, 1], preferred_element_type=jnp.float32)
    prod_im = jnp.einsum(
        form, green_re, sigma[:, :, 1], preferred_element_type=jnp.float32
    ) + jnp.einsum(form, green_im, sigma[:, :, 0], preferred_element_type=jnp.float32)
    prod_re = prod_re.astype(jnp.bfloat16)
    prod_im = prod_im.astype(jnp.bfloat16)
    trans = "esij,eskj->esik"
    out_re = jnp.einsum(trans, prod_re, green_re, preferred_element_type=jnp.float32) - jnp.einsum(
        trans, prod_im, green_im, preferred_element_type=jnp.float32
    )
    out_im = jnp.einsum(trans, prod_re, green_im, preferred_element_type=jnp.float32) + jnp.einsum(
        trans, prod_im, green_re, preferred_element_type=jnp.float32
    )
    result = green0.astype(jnp.float32) + jnp.stack([out_re, out_im], axis=2) / size
    return result.astype(jnp.bfloat16)


def local(green0, coupling):
    green = green0
    for turn in range(ITERS):
        lower = passed_along(green, "energy", OFFSET)
        upper = passed_along(green, "energy", -OFFSET)
        own_sum = (lower.astype(jnp.float32) + upper.astype(jnp.float32)).astype(jnp.bfloat16)
        summed = with_halo(own_sum, (("slab", 1),), 1)
        green = dyson(green0, coupling, summed)
    return green


def solution(mesh):
    placed = (P("energy", "slab", None, None, None), P("slab", None, None, None))
    return jax.shard_map(
        local,
        mesh=mesh,
        in_specs=placed,
        out_specs=P("energy", "slab", None, None, None),
        check_vma=False,
    )
```

profile of v0, /device:TPU:5, one launch (start us, length us, event | category | flops | bytes accessed | tf_op | source)
XLA Modules:
  0.0 103.1 jit_solution(4909289680621403076)
XLA Ops:
  0.0 0.0 copy-start.1
  0.0 1.4 %copy.3 = bf16[1,1,2,384,384]{3,4,2,1,0:T(8,128)(2,1)S(1)} copy(bf16[1,1,2,384,384]{4,3,2,1,0:T(8,128)(2,1)} %param.2) | data formatting | bytes 1179648 | tf_op args[0]
  1.5 5.1 %collective-permute-start = (bf16[1,1,2,384,384]{3,4,2,1,0:T(8,128)(2,1)S(1)}, bf16[1,1,2,384,384]{3,4,2,1,0:T(8,128)(2,1)S(1)}, u32[]{:S(2)}, u32[]{:S(2)}) collective-permute-start(bf16[1,1,2,384,384]{3,4,2,1,0:T(8,128)(2,1)S(1)} %copy.3), channel_id=1, source_target_pairs={{0,14},{2,16},{4,18},{6,20},{8,22},{10,24},{12,26},{14,28},{16,30}... | collective-permute-start | bytes 1769480 | tf_op jit(solution)/shard_map/ppermute | solution.py:13
  6.6 1.3 %collective-permute-start.1 = (bf16[1,1,2,384,384]{3,4,2,1,0:T(8,128)(2,1)S(1)}, bf16[1,1,2,384,384]{3,4,2,1,0:T(8,128)(2,1)S(1)}, u32[]{:S(2)}, u32[]{:S(2)}) collective-permute-start(bf16[1,1,2,384,384]{3,4,2,1,0:T(8,128)(2,1)S(1)} %copy.3), channel_id=1, source_target_pairs={{14,0},{16,2},{18,4},{20,6},{22,8},{24,10},{26,12},{28,14},{30,16}... | collective-permute-start | bytes 1769480 | tf_op jit(solution)/shard_map/ppermute | solution.py:13
  7.9 10.7 %collective-permute-done = bf16[1,1,2,384,384]{3,4,2,1,0:T(8,128)(2,1)S(1)} collective-permute-done((bf16[1,1,2,384,384]{3,4,2,1,0:T(8,128)(2,1)S(1)}, bf16[1,1,2,384,384]{3,4,2,1,0:T(8,128)(2,1)S(1)}, u32[]{:S(2)}, u32[]{:S(2)}) %collective-permute-start) | collective-permute-done | bytes 589856 | tf_op jit(solution)/shard_map/ppermute | solution.py:13
  18.6 19.5 %collective-permute-done.1 = bf16[1,1,2,384,384]{3,4,2,1,0:T(8,128)(2,1)S(1)} collective-permute-done((bf16[1,1,2,384,384]{3,4,2,1,0:T(8,128)(2,1)S(1)}, bf16[1,1,2,384,384]{3,4,2,1,0:T(8,128)(2,1)S(1)}, u32[]{:S(2)}, u32[]{:S(2)}) %collective-permute-start.1) | collective-permute-done | bytes 589856 | tf_op jit(solution)/shard_map/ppermute | solution.py:13
  38.1 0.1 add_convert_fusion.1
  38.2 1.3 %collective-permute-start.2 = (bf16[1,1,2,384,384]{3,4,2,1,0:T(8,128)(2,1)S(1)}, bf16[1,1,2,384,384]{3,4,2,1,0:T(8,128)(2,1)S(1)}, u32[]{:S(2)}, u32[]{:S(2)}) collective-permute-start(bf16[1,1,2,384,384]{3,4,2,1,0:T(8,128)(2,1)S(1)} %add_convert_fusion.1), channel_id=1, source_target_pairs={{0,1},{2,3},{4,5},{6,7},{8,9},{10,11},{12,13},{14,15},{16,17},{18,... | collective-permute-start | bytes 1769480 | tf_op jit(solution)/shard_map/ppermute | solution.py:21
  39.5 4.3 %collective-permute-start.3 = (bf16[1,1,2,384,384]{3,4,2,1,0:T(8,128)(2,1)S(1)}, bf16[1,1,2,384,384]{3,4,2,1,0:T(8,128)(2,1)}, u32[]{:S(2)}, u32[]{:S(2)}) collective-permute-start(bf16[1,1,2,384,384]{3,4,2,1,0:T(8,128)(2,1)S(1)} %add_convert_fusion.1), channel_id=1, source_target_pairs={{1,0},{3,2},{5,4},{7,6},{9,8},{11,10},{13,12},{15,14},{17,16},{19,... | collective-permute-start | bytes 1769480 | tf_op jit(solution)/shard_map/ppermute | solution.py:24
  43.8 0.0 collective-permute-done.2
  43.8 0.0 copy-done.1
  43.8 1.0 %fusion.9 = f32[2,384,384]{2,1,0:T(8,128)S(1)} fusion(bf16[1,1,2,384,384]{3,4,2,1,0:T(8,128)(2,1)S(1)} %collective-permute-done.2, bf16[1,3,384,384]{3,2,1,0:T(8,128)(2,1)S(1)} %copy-done.1), kind=kOutput, calls=%fused_computation.29 | convolution fusion | flops 453279744 | bytes 2359296 | tf_op jit(solution)/shard_map/escij,skj->escik/dot_general | solution.py:39
  44.8 2.1 %convolution_add_fusion.3 = f32[2,384,384]{2,1,0:T(8,128)} fusion(f32[2,384,384]{2,1,0:T(8,128)S(1)} %fusion.9, bf16[1,1,2,384,384]{3,4,2,1,0:T(8,128)(2,1)S(1)} %add_convert_fusion.1, bf16[1,3,384,384]{3,2,1,0:T(8,128)(2,1)S(1)} %copy-done.1), kind=kOutput, calls=%fused_computation.5 | convolution fusion | flops 453574656 | bytes 3538944 | tf_op jit(solution)/shard_map/escij,skj->escik/dot_general | solution.py:39
  46.9 0.0 copy-start
  46.9 0.0 collective-permute-done.3
  46.9 2.5 %fusion.3 = bf16[1,1,2,384,384]{4,3,2,0,1:T(8,128)(2,1)S(1)} fusion(f32[2,384,384]{2,1,0:T(8,128)} %convolution_add_fusion.3, bf16[1,1,2,384,384]{3,4,2,1,0:T(8,128)(2,1)} %collective-permute-done.3, bf16[1,3,384,384]{3,2,1,0:T(8,128)(2,1)S(1)} %copy-done.1), kind=kOutput, calls=%fused_computation.15 | convolution fusion | flops 453869568 | bytes 2949120 | tf_op jit(solution)/shard_map/escij,skj->escik/dot_general | solution.py:39
  49.5 0.0 copy-done
  49.5 0.4 fusion.64
  49.9 0.4 fusion.68
  50.3 0.4 fusion.16
  50.7 0.4 fusion.66
  51.1 0.4 fusion.51
  51.5 0.4 fusion.17
  51.9 0.4 fusion.7
  52.3 0.4 fusion.6
  52.8 0.2 fusion.20
  52.9 1.3 %collective-permute-start.4 = (bf16[1,1,2,384,384]{4,3,2,1,0:T(8,128)(2,1)S(1)}, bf16[1,1,2,384,384]{4,3,2,1,0:T(8,128)(2,1)S(1)}, u32[]{:S(2)}, u32[]{:S(2)}) collective-permute-start(bf16[1,1,2,384,384]{4,3,2,1,0:T(8,128)(2,1)S(1)} %fusion.20), channel_id=1, source_target_pairs={{0,14},{2,16},{4,18},{6,20},{8,22},{10,24},{12,26},{14,28},{16,30}... | collective-permute-start | bytes 1769480 | tf_op jit(solution)/shard_map/ppermute | solution.py:13
  54.3 1.3 %collective-permute-start.5 = (bf16[1,1,2,384,384]{4,3,2,1,0:T(8,128)(2,1)S(1)}, bf16[1,1,2,384,384]{4,3,2,1,0:T(8,128)(2,1)S(1)}, u32[]{:S(2)}, u32[]{:S(2)}) collective-permute-start(bf16[1,1,2,384,384]{4,3,2,1,0:T(8,128)(2,1)S(1)} %fusion.20), channel_id=1, source_target_pairs={{14,0},{16,2},{18,4},{20,6},{22,8},{24,10},{26,12},{28,14},{30,16}... | collective-permute-start | bytes 1769480 | tf_op jit(solution)/shard_map/ppermute | solution.py:13
  55.6 11.0 %collective-permute-done.4 = bf16[1,1,2,384,384]{4,3,2,1,0:T(8,128)(2,1)S(1)} collective-permute-done((bf16[1,1,2,384,384]{4,3,2,1,0:T(8,128)(2,1)S(1)}, bf16[1,1,2,384,384]{4,3,2,1,0:T(8,128)(2,1)S(1)}, u32[]{:S(2)}, u32[]{:S(2)}) %collective-permute-start.4) | collective-permute-done | bytes 589856 | tf_op jit(solution)/shard_map/ppermute | solution.py:13
  66.6 19.4 %collective-permute-done.5 = bf16[1,1,2,384,384]{4,3,2,1,0:T(8,128)(2,1)S(1)} collective-permute-done((bf16[1,1,2,384,384]{4,3,2,1,0:T(8,128)(2,1)S(1)}, bf16[1,1,2,384,384]{4,3,2,1,0:T(8,128)(2,1)S(1)}, u32[]{:S(2)}, u32[]{:S(2)}) %collective-permute-start.5) | collective-permute-done | bytes 589856 | tf_op jit(solution)/shard_map/ppermute | solution.py:13
  86.0 0.1 add_convert_fusion
  86.1 1.3 %collective-permute-start.6 = (bf16[1,1,2,384,384]{4,3,2,1,0:T(8,128)(2,1)S(1)}, bf16[1,1,2,384,384]{4,3,2,1,0:T(8,128)(2,1)}, u32[]{:S(2)}, u32[]{:S(2)}) collective-permute-start(bf16[1,1,2,384,384]{4,3,2,1,0:T(8,128)(2,1)S(1)} %add_convert_fusion), channel_id=1, source_target_pairs={{0,1},{2,3},{4,5},{6,7},{8,9},{10,11},{12,13},{14,15},{16,17},{18,... | collective-permute-start | bytes 1769480 | tf_op jit(solution)/shard_map/ppermute | solution.py:21
  87.4 4.7 %collective-permute-start.7 = (bf16[1,1,2,384,384]{4,3,2,1,0:T(8,128)(2,1)S(1)}, bf16[1,1,2,384,384]{4,3,2,1,0:T(8,128)(2,1)}, u32[]{:S(2)}, u32[]{:S(2)}) collective-permute-start(bf16[1,1,2,384,384]{4,3,2,1,0:T(8,128)(2,1)S(1)} %add_convert_fusion), channel_id=1, source_target_pairs={{1,0},{3,2},{5,4},{7,6},{9,8},{11,10},{13,12},{15,14},{17,16},{19,... | collective-permute-start | bytes 1769480 | tf_op jit(solution)/shard_map/ppermute | solution.py:24
  92.1 0.0 collective-permute-done.6
  92.1 2.1 %fusion.13 = f32[2,384,384]{2,1,0:T(8,128)S(1)} fusion(bf16[1,1,2,384,384]{4,3,2,1,0:T(8,128)(2,1)} %collective-permute-done.6, bf16[1,3,384,384]{3,2,1,0:T(8,128)(2,1)S(1)} %copy-done.1), kind=kOutput, calls=%fused_computation.33 | convolution fusion | flops 453279744 | bytes 2359296 | tf_op jit(solution)/shard_map/escij,skj->escik/dot_general | solution.py:39
  94.2 2.1 %convolution_add_fusion.1 = f32[2,384,384]{2,1,0:T(8,128)} fusion(f32[2,384,384]{2,1,0:T(8,128)S(1)} %fusion.13, bf16[1,1,2,384,384]{4,3,2,1,0:T(8,128)(2,1)S(1)} %add_convert_fusion, bf16[1,3,384,384]{3,2,1,0:T(8,128)(2,1)S(1)} %copy-done.1), kind=kOutput, calls=%fused_computation.3 | convolution fusion | flops 453574656 | bytes 3538944 | tf_op jit(solution)/shard_map/escij,skj->escik/dot_general | solution.py:39
  96.3 0.0 collective-permute-done.7
  96.3 2.5 %fusion.2 = bf16[1,1,2,384,384]{4,3,2,0,1:T(8,128)(2,1)S(1)} fusion(f32[2,384,384]{2,1,0:T(8,128)} %convolution_add_fusion.1, bf16[1,1,2,384,384]{4,3,2,1,0:T(8,128)(2,1)} %collective-permute-done.7, bf16[1,3,384,384]{3,2,1,0:T(8,128)(2,1)S(1)} %copy-done.1), kind=kOutput, calls=%fused_computation.14 | convolution fusion | flops 453869568 | bytes 2949120 | tf_op jit(solution)/shard_map/escij,skj->escik/dot_general | solution.py:39
  98.9 0.4 fusion.57
  99.3 0.4 fusion.61
  99.7 0.4 fusion.18
  100.1 0.4 fusion.59
  100.5 0.4 fusion.46
  100.9 0.4 fusion.19
  101.3 0.4 fusion.5
  101.7 0.4 fusion.4
  102.1 1.0 fusion.21
Async XLA Ops:
  0.0 43.8 %copy-start.1 = (bf16[1,3,384,384]{3,2,1,0:T(8,128)(2,1)S(1)}, bf16[1,3,384,384]{3,2,1,0:T(8,128)(2,1)}, u32[]{:S(2)}) copy-start(bf16[1,3,384,384]{3,2,1,0:T(8,128)(2,1)} %param.3) | copy-start | bytes 2654212
  1.5 17.1 %collective-permute-start = (bf16[1,1,2,384,384]{3,4,2,1,0:T(8,128)(2,1)S(1)}, bf16[1,1,2,384,384]{3,4,2,1,0:T(8,128)(2,1)S(1)}, u32[]{:S(2)}, u32[]{:S(2)}) collective-permute-start(bf16[1,1,2,384,384]{3,4,2,1,0:T(8,128)(2,1)S(1)} %copy.3), channel_id=1, source_target_pairs={{0,14},{2,16},{4,18},{6,20},{8,22},{10,24},{12,26},{14,28},{16,30}... | collective-permute-start | bytes 1769480 | tf_op jit(solution)/shard_map/ppermute | solution.py:13
  6.6 31.5 %collective-permute-start.1 = (bf16[1,1,2,384,384]{3,4,2,1,0:T(8,128)(2,1)S(1)}, bf16[1,1,2,384,384]{3,4,2,1,0:T(8,128)(2,1)S(1)}, u32[]{:S(2)}, u32[]{:S(2)}) collective-permute-start(bf16[1,1,2,384,384]{3,4,2,1,0:T(8,128)(2,1)S(1)} %copy.3), channel_id=1, source_target_pairs={{14,0},{16,2},{18,4},{20,6},{22,8},{24,10},{26,12},{28,14},{30,16}... | collective-permute-start | bytes 1769480 | tf_op jit(solution)/shard_map/ppermute | solution.py:13
  38.2 5.6 %collective-permute-start.2 = (bf16[1,1,2,384,384]{3,4,2,1,0:T(8,128)(2,1)S(1)}, bf16[1,1,2,384,384]{3,4,2,1,0:T(8,128)(2,1)S(1)}, u32[]{:S(2)}, u32[]{:S(2)}) collective-permute-start(bf16[1,1,2,384,384]{3,4,2,1,0:T(8,128)(2,1)S(1)} %add_convert_fusion.1), channel_id=1, source_target_pairs={{0,1},{2,3},{4,5},{6,7},{8,9},{10,11},{12,13},{14,15},{16,17},{18,... | collective-permute-start | bytes 1769480 | tf_op jit(solution)/shard_map/ppermute | solution.py:21
  39.5 7.4 %collective-permute-start.3 = (bf16[1,1,2,384,384]{3,4,2,1,0:T(8,128)(2,1)S(1)}, bf16[1,1,2,384,384]{3,4,2,1,0:T(8,128)(2,1)}, u32[]{:S(2)}, u32[]{:S(2)}) collective-permute-start(bf16[1,1,2,384,384]{3,4,2,1,0:T(8,128)(2,1)S(1)} %add_convert_fusion.1), channel_id=1, source_target_pairs={{1,0},{3,2},{5,4},{7,6},{9,8},{11,10},{13,12},{15,14},{17,16},{19,... | collective-permute-start | bytes 1769480 | tf_op jit(solution)/shard_map/ppermute | solution.py:24
  46.9 2.6 %copy-start = (bf16[1,1,2,384,384]{4,3,2,1,0:T(8,128)(2,1)S(1)}, bf16[1,1,2,384,384]{4,3,2,1,0:T(8,128)(2,1)}, u32[]{:S(2)}) copy-start(bf16[1,1,2,384,384]{4,3,2,1,0:T(8,128)(2,1)} %param.2) | copy-start | bytes 1769476
  52.9 13.6 %collective-permute-start.4 = (bf16[1,1,2,384,384]{4,3,2,1,0:T(8,128)(2,1)S(1)}, bf16[1,1,2,384,384]{4,3,2,1,0:T(8,128)(2,1)S(1)}, u32[]{:S(2)}, u32[]{:S(2)}) collective-permute-start(bf16[1,1,2,384,384]{4,3,2,1,0:T(8,128)(2,1)S(1)} %fusion.20), channel_id=1, source_target_pairs={{0,14},{2,16},{4,18},{6,20},{8,22},{10,24},{12,26},{14,28},{16,30}... | collective-permute-start | bytes 1769480 | tf_op jit(solution)/shard_map/ppermute | solution.py:13
  54.3 31.7 %collective-permute-start.5 = (bf16[1,1,2,384,384]{4,3,2,1,0:T(8,128)(2,1)S(1)}, bf16[1,1,2,384,384]{4,3,2,1,0:T(8,128)(2,1)S(1)}, u32[]{:S(2)}, u32[]{:S(2)}) collective-permute-start(bf16[1,1,2,384,384]{4,3,2,1,0:T(8,128)(2,1)S(1)} %fusion.20), channel_id=1, source_target_pairs={{14,0},{16,2},{18,4},{20,6},{22,8},{24,10},{26,12},{28,14},{30,16}... | collective-permute-start | bytes 1769480 | tf_op jit(solution)/shard_map/ppermute | solution.py:13
  86.1 6.0 %collective-permute-start.6 = (bf16[1,1,2,384,384]{4,3,2,1,0:T(8,128)(2,1)S(1)}, bf16[1,1,2,384,384]{4,3,2,1,0:T(8,128)(2,1)}, u32[]{:S(2)}, u32[]{:S(2)}) collective-permute-start(bf16[1,1,2,384,384]{4,3,2,1,0:T(8,128)(2,1)S(1)} %add_convert_fusion), channel_id=1, source_target_pairs={{0,1},{2,3},{4,5},{6,7},{8,9},{10,11},{12,13},{14,15},{16,17},{18,... | collective-permute-start | bytes 1769480 | tf_op jit(solution)/shard_map/ppermute | solution.py:21
  87.4 8.9 %collective-permute-start.7 = (bf16[1,1,2,384,384]{4,3,2,1,0:T(8,128)(2,1)S(1)}, bf16[1,1,2,384,384]{4,3,2,1,0:T(8,128)(2,1)}, u32[]{:S(2)}, u32[]{:S(2)}) collective-permute-start(bf16[1,1,2,384,384]{4,3,2,1,0:T(8,128)(2,1)S(1)} %add_convert_fusion), channel_id=1, source_target_pairs={{1,0},{3,2},{5,4},{7,6},{9,8},{11,10},{13,12},{15,14},{17,16},{19,... | collective-permute-start | bytes 1769480 | tf_op jit(solution)/shard_map/ppermute | solution.py:24
where the time goes:
time: 103 us
  waiting for transfers between devices  60.6 us (59%)
  starting transfers between devices  20.6 us (20%)
  matrix products  18.8 us (18%)
  local copies, waits for them, and re-layouts  1.46 us (1%)
  other arithmetic  1.41 us (1%)
    ppermute x4, waiting for transfers between devices, passed_along(): lax.ppermute(value, axis, [(source, source + steps) for source in range(f...  60.6 us
    dot_general x6, matrix products, dyson(): jnp.einsum('escij,skj->escik', left, weights, preferred_element_type=jnp....  12.4 us
    ppermute x4, starting transfers between devices, passed_along(): lax.ppermute(value, axis, [(source, source + steps) for source in range(f...  9.03 us
    ppermute x2, starting transfers between devices, with_halo(): lax.ppermute(lax.slice_in_dim(block, 0, width, axis=dim), axis, backward)  8.97 us
    ppermute x2, starting transfers between devices, with_halo(): lax.ppermute(lax.slice_in_dim(block, block.shape[dim] - width, None, axis...  2.58 us
  transfers between devices with their start and end apart: 8, of which 4 were waited for; matrix products, arithmetic and copies ran while one was open for 7% of the time, Pallas kernels for 0%

commit v1 on v0

--- a/solution.py
+++ b/solution.py
@@ -1,10 +1,16 @@
+import functools
+
 import jax
 import jax.numpy as jnp
 from jax import lax
+from jax.experimental import pallas as pl
+from jax.experimental.pallas import tpu as pltpu
 from jax.sharding import PartitionSpec as P
 
 OFFSET = 7
 ITERS = 2
+VMEM_LIMIT = 12 << 20
+LAYER = 4
 
 
 def passed_along(value, axis, steps):
@@ -62,7 +68,7 @@
     return result.astype(jnp.bfloat16)
 
 
-def local(green0, coupling):
+def plain(green0, coupling):
     green = green0
     for turn in range(ITERS):
         lower = passed_along(green, "energy", OFFSET)
@@ -73,7 +79,191 @@
     return green
 
 
+def routes(energies):
+    chains = [list(range(first, energies, OFFSET)) for first in range(min(OFFSET, energies))]
+    threes = [chain for chain in chains if len(chain) == 3]
+    twos = [chain for chain in chains if len(chain) == 2]
+
+    def crossing(one, two):
+        spans = [sorted((end // LAYER for end in flow)) for flow in (one, two)]
+        same_way = (one[1] > one[0]) == (two[1] > two[0])
+        over = max(spans[0][0], spans[1][0]) < min(spans[0][1], spans[1][1])
+        return same_way and over and one[0] % LAYER == two[0] % LAYER
+
+    lower = [(low, mid) for low, mid, _ in threes]
+    upper = [(high, mid) for _, mid, high in threes]
+    pairs = [flow for a, b in twos for flow in ((a, b), (b, a))]
+    late = [flow for flow in pairs if any(crossing(flow, into) for into in lower + upper)]
+    first = lower + [flow for flow in pairs if flow not in late]
+    back = ([(mid, high) for _, mid, high in threes], [(mid, low) for low, mid, _ in threes])
+    return first, upper, late, back
+
+
+def dot(left, right):
+    return jnp.dot(left, right, preferred_element_type=jnp.float32)
+
+
+def dot_t(left, right):
+    return lax.dot_general(
+        left, right, (((1,), (1,)), ((), ())), preferred_element_type=jnp.float32
+    )
+
+
+def self_energy(mine, other, weights, beside):
+    size = mine.shape[-1]
+    own, far = weights[1], weights[beside]
+    near = dot(own, jnp.concatenate([mine[0], mine[1]], axis=1)).astype(jnp.bfloat16)
+    cross = dot(far, jnp.concatenate([other[0], other[1]], axis=1)).astype(jnp.bfloat16)
+    left = jnp.concatenate(
+        [
+            jnp.concatenate([near[:, :size], cross[:, :size]], axis=1),
+            jnp.concatenate([near[:, size:], cross[:, size:]], axis=1),
+        ],
+        axis=0,
+    )
+    return dot_t(left, jnp.concatenate([own, far], axis=1)).astype(jnp.bfloat16)
+
+
+def stepped(green, sigma_re, sigma_im):
+    re, im = green[0], green[1]
+    size = re.shape[0]
+    square = jnp.concatenate(
+        [
+            jnp.concatenate([sigma_re, sigma_im], axis=1),
+            jnp.concatenate([-sigma_im, sigma_re], axis=1),
+        ],
+        axis=0,
+    )
+    product = dot(jnp.concatenate([re, im], axis=1), square).astype(jnp.bfloat16)
+    turned = jnp.concatenate(
+        [jnp.concatenate([re, -im], axis=1), jnp.concatenate([im, re], axis=1)], axis=0
+    )
+    added = dot_t(product, turned)
+    return (
+        re.astype(jnp.float32) + added[:, :size] / size,
+        im.astype(jnp.float32) + added[:, size:] / size,
+    )
+
+
+def sigma_kernel(flags, mine, other, weights, out):
+    size = mine.shape[-1]
+    sigma = self_energy(mine, other, weights, flags[0])
+    out[0] = sigma[:size]
+    out[1] = sigma[size:]
+
+
+def sum_kernel(flags, one, two, out):
+    @pl.when(flags[1] == 1)
+    def _():
+        out[...] = (one[...].astype(jnp.float32) + two[...].astype(jnp.float32)).astype(out.dtype)
+
+
+def pick_kernel(flags, stepped_on, high, low, out):
+    for value, source in enumerate((stepped_on, high, low)):
+
+        @pl.when(flags[4] == value)
+        def _():
+            out[...] = source[...]
+
+
+def centre_kernel(flags, own, mine, other, weights, out):
+    @pl.when(flags[1] == 1)
+    def _():
+        size = own.shape[-1]
+        sigma = self_energy(mine, other, weights, flags[0])
+        out[0], out[1] = (
+            part.astype(jnp.bfloat16) for part in stepped(own, sigma[:size], sigma[size:])
+        )
+
+
+def neighbour_kernel(flags, first, upper, late, sigma, out):
+    @pl.when(flags[1] == 1)
+    def _():
+        below = stepped(first, sigma[0], sigma[1])
+        above = stepped(upper, sigma[0], sigma[1])
+        for part in range(2):
+            one = below[part].astype(jnp.bfloat16).astype(jnp.float32)
+            two = above[part].astype(jnp.bfloat16).astype(jnp.float32)
+            out[part] = (one + two).astype(jnp.bfloat16)
+
+    for flag, source in ((2, first), (3, late)):
+
+        @pl.when(flags[flag] == 1)
+        def _():
+            out[0], out[1] = (
+                part.astype(jnp.bfloat16) for part in stepped(source, sigma[0], sigma[1])
+            )
+
+
+def last_kernel(flags, own, mine, other, weights, out):
+    size = own.shape[-1]
+    sigma = self_energy(mine, other, weights, flags[0])
+    out[0], out[1] = (
+        part.astype(jnp.bfloat16) for part in stepped(own, sigma[:size], sigma[size:])
+    )
+
+
+def call(kernel, flags, *blocks):
+    like = blocks[0]
+    return pl.pallas_call(
+        kernel,
+        out_shape=jax.ShapeDtypeStruct(like.shape, like.dtype),
+        in_specs=[pl.BlockSpec(memory_space=pltpu.SMEM)]
+        + [pl.BlockSpec(memory_space=pltpu.VMEM)] * len(blocks),
+        out_specs=pl.BlockSpec(memory_space=pltpu.VMEM),
+        compiler_params=pltpu.CompilerParams(vmem_limit_bytes=VMEM_LIMIT),
+        name=kernel.__name__,
+    )(flags, *blocks)
+
+
+def chained(first, upper, late, back, green0, coupling):
+    own, weights = green0[0, 0], coupling[0]
+    energy, slab = lax.axis_index("energy"), lax.axis_index("slab")
+    slabs = lax.axis_size("slab")
+
+    def is_in(members):
+        return functools.reduce(
+            jnp.logical_or, [energy == member for member in members], jnp.bool_(False)
+        ).astype(jnp.int32)
+
+    middles = [target for _, target in upper]
+    flags = jnp.stack(
+        [
+            jnp.where(slab == 0, 2, 0).astype(jnp.int32),
+            is_in(middles),
+            is_in([target for _, target in first if target not in middles]),
+            is_in([target for _, target in late]),
+            sum(is_in([target for _, target in flows]) * (i + 1) for i, flows in enumerate(back)),
+        ]
+    )
+
+    def swapped(value, members):
+        flows = [(i * slabs + s, i * slabs + 1 - s) for i in members for s in range(slabs)]
+        return lax.ppermute(value, ("energy", "slab"), flows)
+
+    everyone = range(lax.axis_size("energy"))
+    from_first = lax.ppermute(own, "energy", first)
+    from_upper = lax.ppermute(own, "energy", upper)
+    sigma = call(sigma_kernel, flags, own, swapped(own, everyone), weights)
+    from_first, from_upper, sigma, held = lax.optimization_barrier(
+        (from_first, from_upper, sigma, own)
+    )
+    from_late = lax.ppermute(held, "energy", late)
+    both = call(sum_kernel, flags, from_first, from_upper)
+    centre = call(centre_kernel, flags, own, both, swapped(both, middles), weights)
+    returned = [lax.ppermute(centre, "energy", flows) for flows in back]
+    stepped_on = call(neighbour_kernel, flags, from_first, from_upper, from_late, sigma)
+    green = call(pick_kernel, flags, stepped_on, *returned)
+    out = call(last_kernel, flags, own, green, swapped(green, everyone), weights)
+    return out[None, None]
+
+
 def solution(mesh):
+    energies, slabs = mesh.shape["energy"], mesh.shape["slab"]
+    if OFFSET < energies <= 3 * OFFSET and slabs == 2:
+        local = functools.partial(chained, *routes(energies))
+    else:
+        local = plain
     placed = (P("energy", "slab", None, None, None), P("slab", None, None, None))
     return jax.shard_map(
         local,

time: 103 us -> 67.7 us (0.66)
  the two profiles are of different devices: /device:TPU:5 before, /device:TPU:0 now
where the time goes in v1:
time: 67.7 us; the launch traced here: 67.4 us
  waiting for transfers between devices  45.9 us (68%)
  starting transfers between devices  11 us (16%)
  Pallas kernels  7.98 us (12%)
  local copies, waits for them, and re-layouts  2.33 us (3%)
    ppermute x2, waiting for transfers between devices, chained(): returned = [lax.ppermute(centre, 'energy', flows) for flows in back]  22.9 us
    ppermute x1, waiting for transfers between devices, chained(): from_first = lax.ppermute(own, 'energy', first)  21 us
    pallas_call x6, Pallas kernels, call(): pl.pallas_call(kernel, out_shape=jax.ShapeDtypeStruct(like.shape, like.dt...  7.98 us
    ppermute x1, starting transfers between devices, chained(): from_first = lax.ppermute(own, 'energy', first)  6.38 us
    unnamed x8, local copies, waits for them, and re-layouts  2.25 us
    ppermute x3, waiting for transfers between devices, swapped(): return lax.ppermute(value, ('energy', 'slab'), flows)  2 us
    ppermute x2, starting transfers between devices, chained(): returned = [lax.ppermute(centre, 'energy', flows) for flows in back]  1.99 us
  transfers between devices with their start and end apart: 8, of which 3 were waited for; matrix products, arithmetic and copies ran while one was open for 0% of the time, Pallas kernels for 5%

profile of v1, /device:TPU:0, one launch (start us, length us, event | category | flops | bytes accessed | tf_op | source)
XLA Modules:
  0.0 67.4 jit_solution(14778533241105046636)
XLA Ops:
  0.0 0.5 collective-permute-start.2
  0.5 6.4 %collective-permute-start = (bf16[2,384,384]{2,1,0:T(8,128)(2,1)}, bf16[2,384,384]{2,1,0:T(8,128)(2,1)S(1)}, u32[]{:S(2)}, u32[]{:S(2)}) collective-permute-start(bf16[2,384,384]{2,1,0:T(8,128)(2,1)} %bitcast.12), channel_id=1, source_target_pairs={{0,14},{2,16},{4,18},{18,4},{6,20},{8,22},{22,8},{24,10},{12,26},{... | collective-permute-start | bytes 1769480 | tf_op jit(solution)/shard_map/ppermute | solution.py:245
  6.9 0.7 %collective-permute-start.1 = (bf16[2,384,384]{2,1,0:T(8,128)(2,1)}, bf16[2,384,384]{2,1,0:T(8,128)(2,1)S(1)}, u32[]{:S(2)}, u32[]{:S(2)}) collective-permute-start(bf16[2,384,384]{2,1,0:T(8,128)(2,1)} %bitcast.13), channel_id=1, source_target_pairs={{28,14},{30,16},{29,15},{31,17}} | collective-permute-start | bytes 1769480 | tf_op jit(solution)/shard_map/ppermute | solution.py:246
  7.6 0.1 stack.35.flags
  7.7 0.0 collective-permute-done.2.other
  7.7 0.0 copy-start
  7.7 1.2 %copy-done = bf16[1,3,384,384]{3,2,1,0:T(8,128)(2,1)S(1)} copy-done((bf16[1,3,384,384]{3,2,1,0:T(8,128)(2,1)S(1)}, bf16[1,3,384,384]{3,2,1,0:T(8,128)(2,1)}, u32[]{:S(2)}) %copy-start) | copy-done | bytes 884760
  8.9 0.0 copy-start.2
  8.9 1.1 %copy-done.2 = bf16[1,1,2,384,384]{4,3,2,1,0:T(8,128)(2,1)S(1)} copy-done((bf16[1,1,2,384,384]{4,3,2,1,0:T(8,128)(2,1)S(1)}, bf16[1,1,2,384,384]{4,3,2,1,0:T(8,128)(2,1)}, u32[]{:S(2)}) %copy-start.2) | copy-done | bytes 589848
  10.0 1.9 %sigma_kernel.1.sigma = bf16[2,384,384]{2,1,0:T(8,128)(2,1)S(1)} custom-call(s32[5]{0:T(128)S(1)} %stack.35.flags, bf16[2,384,384]{2,1,0:T(8,128)(2,1)S(1)} %bitcast.14, bf16[2,384,384]{2,1,0:T(8,128)(2,1)S(1)} %collective-permute-done.2.other, bf16[3,384,384]{2,1,0:T(8,128)(2,1)S(1)} %bitcast.8), custom_call_target="tpu_custom_call" | custom-call | tf_op jit(solution)/shard_map/sigma_kernel/pallas_call | solution.py:208
  11.9 0.0 copy-start.3
  11.9 0.0 copy-start.1
  11.9 21.0 %collective-permute-done.first.one = bf16[2,384,384]{2,1,0:T(8,128)(2,1)S(1)} collective-permute-done((bf16[2,384,384]{2,1,0:T(8,128)(2,1)}, bf16[2,384,384]{2,1,0:T(8,128)(2,1)S(1)}, u32[]{:S(2)}, u32[]{:S(2)}) %collective-permute-start) | collective-permute-done | bytes 589856 | tf_op jit(solution)/shard_map/ppermute | solution.py:245
  32.9 0.0 collective-permute-done.1.upper.two
  32.9 0.5 sum_kernel.1.mine
  33.5 0.7 %collective-permute-start.4 = (bf16[2,384,384]{2,1,0:T(8,128)(2,1)S(1)}, bf16[2,384,384]{2,1,0:T(8,128)(2,1)S(1)}, u32[]{:S(2)}, u32[]{:S(2)}) collective-permute-start(bf16[2,384,384]{2,1,0:T(8,128)(2,1)S(1)} %sum_kernel.1.mine), channel_id=1, source_target_pairs={{14,15},{15,14},{16,17},{17,16}} | collective-permute-start | bytes 1769480 | tf_op jit(solution)/shard_map/ppermute | solution.py:242
  34.2 0.0 copy-done.3
  34.2 0.7 %collective-permute-start.3 = (bf16[2,384,384]{2,1,0:T(8,128)(2,1)S(1)}, bf16[2,384,384]{2,1,0:T(8,128)(2,1)S(1)}, u32[]{:S(2)}, u32[]{:S(2)}) collective-permute-start(bf16[2,384,384]{2,1,0:T(8,128)(2,1)S(1)} %bitcast.15), channel_id=1, source_target_pairs={{20,6},{10,24},{21,7},{11,25}} | collective-permute-start | bytes 1769480 | tf_op jit(solution)/shard_map/ppermute | solution.py:251
  34.9 0.0 collective-permute-done.4.other
  34.9 0.0 copy-done.1
  34.9 0.6 centre_kernel.1
  35.5 0.7 %collective-permute-start.5 = (bf16[2,384,384]{2,1,0:T(8,128)(2,1)S(1)}, bf16[2,384,384]{2,1,0:T(8,128)(2,1)S(1)}, u32[]{:S(2)}, u32[]{:S(2)}) collective-permute-start(bf16[2,384,384]{2,1,0:T(8,128)(2,1)S(1)} %centre_kernel.1), channel_id=1, source_target_pairs={{14,28},{16,30},{15,29},{17,31}} | collective-permute-start | bytes 1769480 | tf_op jit(solution)/shard_map/ppermute | solution.py:254
  36.2 1.3 %collective-permute-start.6 = (bf16[2,384,384]{2,1,0:T(8,128)(2,1)S(1)}, bf16[2,384,384]{2,1,0:T(8,128)(2,1)S(1)}, u32[]{:S(2)}, u32[]{:S(2)}) collective-permute-start(bf16[2,384,384]{2,1,0:T(8,128)(2,1)S(1)} %centre_kernel.1), channel_id=1, source_target_pairs={{14,0},{16,2},{15,1},{17,3}} | collective-permute-start | bytes 1769480 | tf_op jit(solution)/shard_map/ppermute | solution.py:254
  37.5 0.0 collective-permute-done.3.late
  37.5 0.6 neighbour_kernel.1.stepped_on
  38.1 0.0 collective-permute-done.5.high
  38.1 22.9 %collective-permute-done.6.low = bf16[2,384,384]{2,1,0:T(8,128)(2,1)S(1)} collective-permute-done((bf16[2,384,384]{2,1,0:T(8,128)(2,1)S(1)}, bf16[2,384,384]{2,1,0:T(8,128)(2,1)S(1)}, u32[]{:S(2)}, u32[]{:S(2)}) %collective-permute-start.6) | collective-permute-done | bytes 589856 | tf_op jit(solution)/shard_map/ppermute | solution.py:254
  61.0 0.6 pick_kernel.1.mine
  61.6 0.1 collective-permute-start.7
  61.7 2.0 %collective-permute-done.7.other = bf16[2,384,384]{2,1,0:T(8,128)(2,1)S(1)} collective-permute-done((bf16[2,384,384]{2,1,0:T(8,128)(2,1)S(1)}, bf16[2,384,384]{2,1,0:T(8,128)(2,1)S(1)}, u32[]{:S(2)}, u32[]{:S(2)}) %collective-permute-start.7) | collective-permute-done | bytes 589856 | tf_op jit(solution)/shard_map/ppermute | solution.py:242
  63.7 3.8 %last_kernel.1 = bf16[2,384,384]{2,1,0:T(8,128)(2,1)} custom-call(s32[5]{0:T(128)S(1)} %stack.35.flags, bf16[2,384,384]{2,1,0:T(8,128)(2,1)S(1)} %bitcast.17, bf16[2,384,384]{2,1,0:T(8,128)(2,1)S(1)} %pick_kernel.1.mine, bf16[2,384,384]{2,1,0:T(8,128)(2,1)S(1)} %collective-permute-done.7.other, bf16[3,384,384]{2,1,0:T(8,128)(2,1)S(1)} %bitcast.10), custom_call_target="tpu_custom_call" | custom-call | tf_op jit(solution)/shard_map/last_kernel/pallas_call | solution.py:208
Async XLA Ops:
  0.0 7.7 %collective-permute-start.2 = (bf16[2,384,384]{2,1,0:T(8,128)(2,1)}, bf16[2,384,384]{2,1,0:T(8,128)(2,1)S(1)}, u32[]{:S(2)}, u32[]{:S(2)}) collective-permute-start(bf16[2,384,384]{2,1,0:T(8,128)(2,1)} %bitcast.11), channel_id=1, source_target_pairs={{0,1},{1,0},{2,3},{3,2},{4,5},{5,4},{6,7},{7,6},{8,9},{9,8},{10,11... | collective-permute-start | bytes 1769480 | tf_op jit(solution)/shard_map/ppermute | solution.py:242
  0.5 32.4 %collective-permute-start = (bf16[2,384,384]{2,1,0:T(8,128)(2,1)}, bf16[2,384,384]{2,1,0:T(8,128)(2,1)S(1)}, u32[]{:S(2)}, u32[]{:S(2)}) collective-permute-start(bf16[2,384,384]{2,1,0:T(8,128)(2,1)} %bitcast.12), channel_id=1, source_target_pairs={{0,14},{2,16},{4,18},{18,4},{6,20},{8,22},{22,8},{24,10},{12,26},{... | collective-permute-start | bytes 1769480 | tf_op jit(solution)/shard_map/ppermute | solution.py:245
  6.9 26.0 %collective-permute-start.1 = (bf16[2,384,384]{2,1,0:T(8,128)(2,1)}, bf16[2,384,384]{2,1,0:T(8,128)(2,1)S(1)}, u32[]{:S(2)}, u32[]{:S(2)}) collective-permute-start(bf16[2,384,384]{2,1,0:T(8,128)(2,1)} %bitcast.13), channel_id=1, source_target_pairs={{28,14},{30,16},{29,15},{31,17}} | collective-permute-start | bytes 1769480 | tf_op jit(solution)/shard_map/ppermute | solution.py:246
  7.7 1.2 %copy-start = (bf16[1,3,384,384]{3,2,1,0:T(8,128)(2,1)S(1)}, bf16[1,3,384,384]{3,2,1,0:T(8,128)(2,1)}, u32[]{:S(2)}) copy-start(bf16[1,3,384,384]{3,2,1,0:T(8,128)(2,1)} %param.3) | copy-start | bytes 2654212
  8.9 1.1 %copy-start.2 = (bf16[1,1,2,384,384]{4,3,2,1,0:T(8,128)(2,1)S(1)}, bf16[1,1,2,384,384]{4,3,2,1,0:T(8,128)(2,1)}, u32[]{:S(2)}) copy-start(bf16[1,1,2,384,384]{4,3,2,1,0:T(8,128)(2,1)} %param.2) | copy-start | bytes 1769476
  11.9 22.3 %copy-start.3 = (bf16[1,1,2,384,384]{4,3,2,1,0:T(8,128)(2,1)S(1)}, bf16[1,1,2,384,384]{4,3,2,1,0:T(8,128)(2,1)}, u32[]{:S(2)}) copy-start(bf16[1,1,2,384,384]{4,3,2,1,0:T(8,128)(2,1)} %param.2) | copy-start | bytes 1769476
  11.9 23.0 %copy-start.1 = (bf16[1,3,384,384]{3,2,1,0:T(8,128)(2,1)S(1)}, bf16[1,3,384,384]{3,2,1,0:T(8,128)(2,1)}, u32[]{:S(2)}) copy-start(bf16[1,3,384,384]{3,2,1,0:T(8,128)(2,1)} %param.3) | copy-start | bytes 2654212
  33.5 1.4 %collective-permute-start.4 = (bf16[2,384,384]{2,1,0:T(8,128)(2,1)S(1)}, bf16[2,384,384]{2,1,0:T(8,128)(2,1)S(1)}, u32[]{:S(2)}, u32[]{:S(2)}) collective-permute-start(bf16[2,384,384]{2,1,0:T(8,128)(2,1)S(1)} %sum_kernel.1.mine), channel_id=1, source_target_pairs={{14,15},{15,14},{16,17},{17,16}} | collective-permute-start | bytes 1769480 | tf_op jit(solution)/shard_map/ppermute | solution.py:242
  34.2 3.3 %collective-permute-start.3 = (bf16[2,384,384]{2,1,0:T(8,128)(2,1)S(1)}, bf16[2,384,384]{2,1,0:T(8,128)(2,1)S(1)}, u32[]{:S(2)}, u32[]{:S(2)}) collective-permute-start(bf16[2,384,384]{2,1,0:T(8,128)(2,1)S(1)} %bitcast.15), channel_id=1, source_target_pairs={{20,6},{10,24},{21,7},{11,25}} | collective-permute-start | bytes 1769480 | tf_op jit(solution)/shard_map/ppermute | solution.py:251
  35.5 2.6 %collective-permute-start.5 = (bf16[2,384,384]{2,1,0:T(8,128)(2,1)S(1)}, bf16[2,384,384]{2,1,0:T(8,128)(2,1)S(1)}, u32[]{:S(2)}, u32[]{:S(2)}) collective-permute-start(bf16[2,384,384]{2,1,0:T(8,128)(2,1)S(1)} %centre_kernel.1), channel_id=1, source_target_pairs={{14,28},{16,30},{15,29},{17,31}} | collective-permute-start | bytes 1769480 | tf_op jit(solution)/shard_map/ppermute | solution.py:254
  36.2 24.8 %collective-permute-start.6 = (bf16[2,384,384]{2,1,0:T(8,128)(2,1)S(1)}, bf16[2,384,384]{2,1,0:T(8,128)(2,1)S(1)}, u32[]{:S(2)}, u32[]{:S(2)}) collective-permute-start(bf16[2,384,384]{2,1,0:T(8,128)(2,1)S(1)} %centre_kernel.1), channel_id=1, source_target_pairs={{14,0},{16,2},{15,1},{17,3}} | collective-permute-start | bytes 1769480 | tf_op jit(solution)/shard_map/ppermute | solution.py:254
  61.6 2.1 %collective-permute-start.7 = (bf16[2,384,384]{2,1,0:T(8,128)(2,1)S(1)}, bf16[2,384,384]{2,1,0:T(8,128)(2,1)S(1)}, u32[]{:S(2)}, u32[]{:S(2)}) collective-permute-start(bf16[2,384,384]{2,1,0:T(8,128)(2,1)S(1)} %pick_kernel.1.mine), channel_id=1, source_target_pairs={{0,1},{1,0},{2,3},{3,2},{4,5},{5,4},{6,7},{7,6},{8,9},{9,8},{10,11... | collective-permute-start | bytes 1769480 | tf_op jit(solution)/shard_map/ppermute | solution.py:242

commit v2 on v0

--- a/solution.py
+++ b/solution.py
@@ -1,10 +1,16 @@
+import functools
+
 import jax
 import jax.numpy as jnp
 from jax import lax
+from jax.experimental import pallas as pl
+from jax.experimental.pallas import tpu as pltpu
 from jax.sharding import PartitionSpec as P
 
 OFFSET = 7
 ITERS = 2
+VMEM_LIMIT = 12 << 20
+ROW, LAYER = 2, 4
 
 
 def passed_along(value, axis, steps):
@@ -62,9 +68,9 @@
     return result.astype(jnp.bfloat16)
 
 
-def local(green0, coupling):
+def plain(green0, coupling):
     green = green0
-    for turn in range(ITERS):
+    for _ in range(ITERS):
         lower = passed_along(green, "energy", OFFSET)
         upper = passed_along(green, "energy", -OFFSET)
         own_sum = (lower.astype(jnp.float32) + upper.astype(jnp.float32)).astype(jnp.bfloat16)
@@ -73,7 +79,250 @@
     return green
 
 
+def links(source, target):
+    passed, at = [], source
+    for step, size in ((LAYER, None), (1, ROW), (ROW, LAYER)):
+        here, there = ((e // step if size is None else e % size // step) for e in (at, target))
+        for _ in range(abs(there - here)):
+            to = at + (step if there > here else -step)
+            passed.append((at, to))
+            at = to
+    return passed
+
+
+def planned(energies):
+    chains = [list(range(first, energies, OFFSET)) for first in range(min(OFFSET, energies))]
+    threes = [chain for chain in chains if len(chain) == 3]
+    twos = [chain for chain in chains if len(chain) == 2]
+    if len(threes) != 2 or len(threes) + len(twos) != len(chains):
+        return None
+    (low0, mid0, high0), (low1, mid1, high1) = threes
+    inward = [(low0, mid0), (low1, mid1), (high0, mid0), (high1, mid1)]
+    plan = {
+        "first": inward[:2],
+        "other": inward[2:],
+        "ends": [(low0, low1), (low1, low0), (high0, high1), (high1, high0)],
+        "second": [(mid0, low0), (mid1, low1), (low0, mid1), (low1, mid0)],
+        "third": [(mid0, high0), (mid1, high1)],
+        "inner": [(high0, mid1), (high1, mid0)],
+    }
+    busy = {link for flow in inward for link in links(*flow)}
+    taken = {link for flow in plan["ends"] for link in links(*flow)}
+    direct, late, relays = [], [], []
+    for source, target in [flow for a, b in twos for flow in ((a, b), (b, a))]:
+        passed = set(links(source, target))
+        relay = target - target % LAYER + source % LAYER
+        if passed & taken or any(abs(a - b) == LAYER for a, b in passed & busy):
+            plan["second"].append((source, target))
+            late.append((source, target))
+        elif passed & busy:
+            plan["other"].append((source, relay))
+            plan["second"].append((relay, target))
+            relays.append((relay, target))
+            taken |= set(links(source, relay))
+        else:
+            plan["first"].append((source, target))
+            direct.append(target)
+            taken |= passed
+    for flows in plan.values():
+        sources, targets = zip(*flows)
+        if len(set(sources)) < len(flows) or len(set(targets)) < len(flows):
+            return None
+    plan["lows"], plan["mids"], plan["highs"] = ([a, b] for a, b in zip(*threes))
+    plan["direct"] = direct
+    plan["relayed"] = [relay for relay, _ in relays]
+    plan["late"] = [source for source, _ in late]
+    plan["second_pairs"] = [target for _, target in late + relays]
+    return plan
+
+
+def dot(left, right):
+    return jnp.dot(left, right, preferred_element_type=jnp.float32)
+
+
+def dot_t(left, right):
+    return lax.dot_general(
+        left, right, (((1,), (1,)), ((), ())), preferred_element_type=jnp.float32
+    )
+
+
+def among(members):
+    energy = lax.axis_index("energy")
+    return functools.reduce(jnp.logical_or, [energy == member for member in members])
+
+
+def self_energy(mine, other, weights):
+    size = mine.shape[-1]
+    own, far = weights[1], weights[2 - 2 * lax.axis_index("slab")]
+    near = dot(own, jnp.concatenate([mine[0], mine[1]], axis=1)).astype(jnp.bfloat16)
+    cross = dot(far, jnp.concatenate([other[0], other[1]], axis=1)).astype(jnp.bfloat16)
+    left = jnp.concatenate(
+        [
+            jnp.concatenate([near[:, :size], cross[:, :size]], axis=1),
+            jnp.concatenate([near[:, size:], cross[:, size:]], axis=1),
+        ],
+        axis=0,
+    )
+    return dot_t(left, jnp.concatenate([own, far], axis=1)).astype(jnp.bfloat16)
+
+
+def stepped(green, sigma_re, sigma_im):
+    re, im = green[0], green[1]
+    size = re.shape[0]
+    square = jnp.concatenate(
+        [
+            jnp.concatenate([sigma_re, sigma_im], axis=1),
+            jnp.concatenate([-sigma_im, sigma_re], axis=1),
+        ],
+        axis=0,
+    )
+    product = dot(jnp.concatenate([re, im], axis=1), square).astype(jnp.bfloat16)
+    turned = jnp.concatenate(
+        [jnp.concatenate([re, -im], axis=1), jnp.concatenate([im, re], axis=1)], axis=0
+    )
+    added = dot_t(product, turned)
+    return (
+        re.astype(jnp.float32) + added[:, :size] / size,
+        im.astype(jnp.float32) + added[:, size:] / size,
+    )
+
+
+def put(out, parts):
+    for part, value in enumerate(parts):
+        out[part] = value.astype(out.dtype)
+
+
+def added(one, two):
+    return (one.astype(jnp.float32) + two.astype(jnp.float32)).astype(one.dtype)
+
+
+def load_kernel(own, weights, own_out, weights_out, sems):
+    copies = [
+        pltpu.make_async_copy(own, own_out, sems.at[0]),
+        pltpu.make_async_copy(weights, weights_out, sems.at[1]),
+    ]
+    for copy in copies:
+        copy.start()
+    for copy in copies:
+        copy.wait()
+
+
+def loaded(*blocks):
+    return pl.pallas_call(
+        load_kernel,
+        out_shape=[jax.ShapeDtypeStruct(block.shape, block.dtype) for block in blocks],
+        in_specs=[pl.BlockSpec(memory_space=pltpu.HBM)] * len(blocks),
+        out_specs=[pl.BlockSpec(memory_space=pltpu.VMEM)] * len(blocks),
+        scratch_shapes=[pltpu.SemaphoreType.DMA((len(blocks),))],
+        compiler_params=pltpu.CompilerParams(vmem_limit_bytes=VMEM_LIMIT),
+        name="load_kernel",
+    )(*(pltpu.with_memory_space_constraint(block, pltpu.HBM) for block in blocks))
+
+
+def first_kernel(plan, own, beside, weights, send):
+    size = own.shape[-1]
+    is_end = among(plan["lows"] + plan["highs"])
+
+    @pl.when(is_end)
+    def _():
+        sigma = self_energy(own, beside, weights)
+        send[0] = sigma[:size]
+        send[1] = sigma[size:]
+
+    @pl.when(jnp.logical_not(is_end))
+    def _():
+        send[...] = own[...]
+
+
+def sigma_kernel(plan, own, beside, weights, sigma_out):
+    size = own.shape[-1]
+
+    @pl.when(jnp.logical_not(among(plan["lows"] + plan["highs"])))
+    def _():
+        sigma = self_energy(own, beside, weights)
+        sigma_out[0] = sigma[:size]
+        sigma_out[1] = sigma[size:]
+
+
+def second_kernel(plan, own, first, other, ends, send):
+    @pl.when(among(plan["mids"]))
+    def _():
+        sigma = [added(first[part], other[part]) for part in range(2)]
+        put(send, stepped(own, *sigma))
+
+    for members, source in (
+        (plan["relayed"], other),
+        (plan["late"], own),
+        (plan["lows"], ends),
+    ):
+
+        @pl.when(among(members))
+        def _():
+            send[...] = source[...]
+
+
+def neighbour_kernel(plan, first, second, third, inner, sigma, out):
+    @pl.when(among(plan["mids"]))
+    def _():
+        steps = [stepped(block, sigma[0], sigma[1]) for block in (second, inner)]
+        put(out, [added(*(step[part].astype(out.dtype) for step in steps)) for part in range(2)])
+
+    for members, source in ((plan["direct"], first), (plan["second_pairs"], second)):
+
+        @pl.when(among(members))
+        def _():
+            put(out, stepped(source, sigma[0], sigma[1]))
+
+    for members, source in ((plan["lows"], second), (plan["highs"], third)):
+
+        @pl.when(among(members))
+        def _():
+            out[...] = source[...]
+
+
+def last_kernel(plan, own, mine, other, weights, out):
+    size = own.shape[-1]
+    sigma = self_energy(mine, other, weights)
+    put(out, stepped(own, sigma[:size], sigma[size:]))
+
+
+def call(kernel, plan, *blocks):
+    space = pl.BlockSpec(memory_space=pltpu.VMEM)
+    return pl.pallas_call(
+        functools.partial(kernel, plan),
+        out_shape=jax.ShapeDtypeStruct(blocks[0].shape, blocks[0].dtype),
+        in_specs=[space] * len(blocks),
+        out_specs=space,
+        compiler_params=pltpu.CompilerParams(vmem_limit_bytes=VMEM_LIMIT),
+    )(*blocks)
+
+
+def chained(plan, green0, coupling):
+    own, weights = green0[0, 0], coupling[0]
+    slabs = lax.axis_size("slab")
+
+    def sent(value, flows):
+        return lax.ppermute(value, "energy", plan[flows])
+
+    def swapped(value):
+        return lax.ppermute(value, "slab", [(s, slabs - 1 - s) for s in range(slabs)])
+
+    beside = swapped(own)
+    own, weights = loaded(own, weights)
+    send = call(first_kernel, plan, own, beside, weights)
+    ends, other, first = sent(own, "ends"), sent(send, "other"), sent(send, "first")
+    inner = sent(ends, "inner")
+    sigma = call(sigma_kernel, plan, own, beside, weights)
+    send = call(second_kernel, plan, own, first, other, ends)
+    second, third = sent(send, "second"), sent(send, "third")
+    green = call(neighbour_kernel, plan, first, second, third, inner, sigma)
+    out = call(last_kernel, plan, own, green, swapped(green), weights)
+    return out[None, None]
+
+
 def solution(mesh):
+    plan = planned(mesh.shape["energy"]) if mesh.shape["slab"] == 2 else None
+    local = functools.partial(chained, plan) if plan else plain
     placed = (P("energy", "slab", None, None, None), P("slab", None, None, None))
     return jax.shard_map(
         local,

time: 103 us -> 52.1 us (0.51)
  the two profiles are of different devices: /device:TPU:5 before, /device:TPU:15 now
where the time goes in v2:
time: 52.1 us; the launch traced here: 51.8 us
  waiting for transfers between devices  31.5 us (60%)
  starting transfers between devices  10.7 us (21%)
  Pallas kernels  9.47 us (18%)
    ppermute x6, waiting for transfers between devices, sent(): return lax.ppermute(value, 'energy', plan[flows])  29.9 us
    pallas_call x5, Pallas kernels, call(): pl.pallas_call(functools.partial(kernel, plan), out_shape=jax.ShapeDtypeS...  8.11 us
    ppermute x6, starting transfers between devices, sent(): return lax.ppermute(value, 'energy', plan[flows])  7.82 us
    ppermute x2, starting transfers between devices, swapped(): lax.ppermute(value, 'slab', [(s, slabs - 1 - s) for s in range(slabs)])  2.87 us
    ppermute x2, waiting for transfers between devices, swapped(): lax.ppermute(value, 'slab', [(s, slabs - 1 - s) for s in range(slabs)])  1.63 us
    pallas_call x1, Pallas kernels, loaded(): pl.pallas_call(load_kernel, out_shape=[jax.ShapeDtypeStruct(block.shape,...  1.36 us
  transfers between devices with their start and end apart: 8, of which 5 were waited for; matrix products, arithmetic and copies ran while one was open for 0% of the time, Pallas kernels for 8%

profile of v2, /device:TPU:15, one launch (start us, length us, event | category | flops | bytes accessed | tf_op | source)
XLA Modules:
  0.0 51.8 jit_solution(8300719915977485546)
XLA Ops:
  0.0 0.7 %collective-permute-start = (bf16[2,384,384]{2,1,0:T(8,128)(2,1)}, bf16[2,384,384]{2,1,0:T(8,128)(2,1)S(1)}, u32[]{:S(2)}, u32[]{:S(2)}) collective-permute-start(bf16[2,384,384]{2,1,0:T(8,128)(2,1)} %bitcast.4), channel_id=1, source_target_pairs={{0,1},{1,0},{2,3},{3,2},{4,5},{5,4},{6,7},{7,6},{8,9},{9,8},{10,11... | collective-permute-start | bytes 1769480 | tf_op jit(solution)/shard_map/ppermute | solution.py:308
  0.7 1.4 %load_kernel.1 = (bf16[2,384,384]{2,1,0:T(8,128)(2,1)S(1)}, bf16[3,384,384]{2,1,0:T(8,128)(2,1)S(1)}) custom-call(bf16[2,384,384]{2,1,0:T(8,128)(2,1)} %bitcast.5, bf16[3,384,384]{2,1,0:T(8,128)(2,1)} %bitcast.3), custom_call_target="tpu_custom_call" | custom-call | tf_op jit(solution)/shard_map/load_kernel/pallas_call | solution.py:211
  2.0 0.7 %collective-permute-start.3 = (bf16[2,384,384]{2,1,0:T(8,128)(2,1)S(1)}, bf16[2,384,384]{2,1,0:T(8,128)(2,1)S(1)}, u32[]{:S(2)}, u32[]{:S(2)}) collective-permute-start(bf16[2,384,384]{2,1,0:T(8,128)(2,1)S(1)} %get-tuple-element.7.own), channel_id=1, source_target_pairs={{0,2},{2,0},{28,30},{30,28},{1,3},{3,1},{29,31},{31,29}} | collective-permute-start | bytes 1769480 | tf_op jit(solution)/shard_map/ppermute | solution.py:305
  2.8 0.0 collective-permute-done.beside
  2.8 0.1 shard_map.28
  2.8 1.3 %collective-permute-start.2 = (bf16[2,384,384]{2,1,0:T(8,128)(2,1)S(1)}, bf16[2,384,384]{2,1,0:T(8,128)(2,1)S(1)}, u32[]{:S(2)}, u32[]{:S(2)}) collective-permute-start(bf16[2,384,384]{2,1,0:T(8,128)(2,1)S(1)} %shard_map.28), channel_id=1, source_target_pairs={{28,14},{30,16},{6,22},{24,8},{29,15},{31,17},{7,23},{25,9}} | collective-permute-start | bytes 1769480 | tf_op jit(solution)/shard_map/ppermute | solution.py:305
  4.1 1.3 %collective-permute-start.1 = (bf16[2,384,384]{2,1,0:T(8,128)(2,1)S(1)}, bf16[2,384,384]{2,1,0:T(8,128)(2,1)S(1)}, u32[]{:S(2)}, u32[]{:S(2)}) collective-permute-start(bf16[2,384,384]{2,1,0:T(8,128)(2,1)S(1)} %shard_map.28), channel_id=1, source_target_pairs={{0,14},{2,16},{4,18},{8,22},{22,8},{26,12},{1,15},{3,17},{5,19},{9... | collective-permute-start | bytes 1769480 | tf_op jit(solution)/shard_map/ppermute | solution.py:305
  5.4 0.0 collective-permute-done.3.ends
  5.5 1.3 %collective-permute-start.6 = (bf16[2,384,384]{2,1,0:T(8,128)(2,1)S(1)}, bf16[2,384,384]{2,1,0:T(8,128)(2,1)S(1)}, u32[]{:S(2)}, u32[]{:S(2)}) collective-permute-start(bf16[2,384,384]{2,1,0:T(8,128)(2,1)S(1)} %collective-permute-done.3.ends), channel_id=1, source_target_pairs={{28,16},{30,14},{29,17},{31,15}} | collective-permute-start | bytes 1769480 | tf_op jit(solution)/shard_map/ppermute | solution.py:305
  6.8 16.8 %collective-permute-done.2.other = bf16[2,384,384]{2,1,0:T(8,128)(2,1)S(1)} collective-permute-done((bf16[2,384,384]{2,1,0:T(8,128)(2,1)S(1)}, bf16[2,384,384]{2,1,0:T(8,128)(2,1)S(1)}, u32[]{:S(2)}, u32[]{:S(2)}) %collective-permute-start.2) | collective-permute-done | bytes 589856 | tf_op jit(solution)/shard_map/ppermute | solution.py:305
  23.6 0.0 collective-permute-done.1.first
  23.6 1.3 %shard_map.29 = bf16[2,384,384]{2,1,0:T(8,128)(2,1)S(1)} custom-call(bf16[2,384,384]{2,1,0:T(8,128)(2,1)S(1)} %get-tuple-element.7.own, bf16[2,384,384]{2,1,0:T(8,128)(2,1)S(1)} %collective-permute-done.1.first, bf16[2,384,384]{2,1,0:T(8,128)(2,1)S(1)} %collective-permute-done.2.other, bf16[2,384,384]{2,1,0:T(8,128)(2,1)S(1)} %collective-permute-done.3.ends), custom_call_target="tpu_custom_call" | custom-call | tf_op jit(solution)/shard_map/pallas_call | solution.py:291
  24.8 1.3 %collective-permute-start.5 = (bf16[2,384,384]{2,1,0:T(8,128)(2,1)S(1)}, bf16[2,384,384]{2,1,0:T(8,128)(2,1)S(1)}, u32[]{:S(2)}, u32[]{:S(2)}) collective-permute-start(bf16[2,384,384]{2,1,0:T(8,128)(2,1)S(1)} %shard_map.29), channel_id=1, source_target_pairs={{14,28},{16,30},{15,29},{17,31}} | collective-permute-start | bytes 1769480 | tf_op jit(solution)/shard_map/ppermute | solution.py:305
  26.2 1.9 %collective-permute-start.4 = (bf16[2,384,384]{2,1,0:T(8,128)(2,1)S(1)}, bf16[2,384,384]{2,1,0:T(8,128)(2,1)S(1)}, u32[]{:S(2)}, u32[]{:S(2)}) collective-permute-start(bf16[2,384,384]{2,1,0:T(8,128)(2,1)S(1)} %shard_map.29), channel_id=1, source_target_pairs={{14,0},{16,2},{0,16},{2,14},{18,4},{22,20},{20,6},{10,24},{8,10},{... | collective-permute-start | bytes 1769480 | tf_op jit(solution)/shard_map/ppermute | solution.py:305
  28.1 1.4 %shard_map.30.sigma = bf16[2,384,384]{2,1,0:T(8,128)(2,1)S(1)} custom-call(bf16[2,384,384]{2,1,0:T(8,128)(2,1)S(1)} %get-tuple-element.7.own, bf16[2,384,384]{2,1,0:T(8,128)(2,1)S(1)} %collective-permute-done.beside, bf16[3,384,384]{2,1,0:T(8,128)(2,1)S(1)} %get-tuple-element.8.weights), custom_call_target="tpu_custom_call" | custom-call | tf_op jit(solution)/shard_map/pallas_call | solution.py:291
  29.5 5.7 %collective-permute-done.6.inner = bf16[2,384,384]{2,1,0:T(8,128)(2,1)S(1)} collective-permute-done((bf16[2,384,384]{2,1,0:T(8,128)(2,1)S(1)}, bf16[2,384,384]{2,1,0:T(8,128)(2,1)S(1)}, u32[]{:S(2)}, u32[]{:S(2)}) %collective-permute-start.6) | collective-permute-done | bytes 589856 | tf_op jit(solution)/shard_map/ppermute | solution.py:305
  35.2 2.6 %collective-permute-done.5.third = bf16[2,384,384]{2,1,0:T(8,128)(2,1)S(1)} collective-permute-done((bf16[2,384,384]{2,1,0:T(8,128)(2,1)S(1)}, bf16[2,384,384]{2,1,0:T(8,128)(2,1)S(1)}, u32[]{:S(2)}, u32[]{:S(2)}) %collective-permute-start.5) | collective-permute-done | bytes 589856 | tf_op jit(solution)/shard_map/ppermute | solution.py:305
  37.8 4.8 %collective-permute-done.4.second = bf16[2,384,384]{2,1,0:T(8,128)(2,1)S(1)} collective-permute-done((bf16[2,384,384]{2,1,0:T(8,128)(2,1)S(1)}, bf16[2,384,384]{2,1,0:T(8,128)(2,1)S(1)}, u32[]{:S(2)}, u32[]{:S(2)}) %collective-permute-start.4) | collective-permute-done | bytes 589856 | tf_op jit(solution)/shard_map/ppermute | solution.py:305
  42.6 2.2 %shard_map.31.mine = bf16[2,384,384]{2,1,0:T(8,128)(2,1)S(1)} custom-call(bf16[2,384,384]{2,1,0:T(8,128)(2,1)S(1)} %collective-permute-done.1.first, bf16[2,384,384]{2,1,0:T(8,128)(2,1)S(1)} %collective-permute-done.4.second, bf16[2,384,384]{2,1,0:T(8,128)(2,1)S(1)} %collective-permute-done.5.third, bf16[2,384,384]{2,1,0:T(8,128)(2,1)S(1)} %collective-permute-done.6.inner, ...), custom_call_target="tpu_custom_call" | custom-call | tf_op jit(solution)/shard_map/pallas_call | solution.py:291
  44.8 2.2 %collective-permute-start.7 = (bf16[2,384,384]{2,1,0:T(8,128)(2,1)S(1)}, bf16[2,384,384]{2,1,0:T(8,128)(2,1)S(1)}, u32[]{:S(2)}, u32[]{:S(2)}) collective-permute-start(bf16[2,384,384]{2,1,0:T(8,128)(2,1)S(1)} %shard_map.31.mine), channel_id=1, source_target_pairs={{0,1},{1,0},{2,3},{3,2},{4,5},{5,4},{6,7},{7,6},{8,9},{9,8},{10,11... | collective-permute-start | bytes 1769480 | tf_op jit(solution)/shard_map/ppermute | solution.py:308
  46.9 1.6 %collective-permute-done.7.other = bf16[2,384,384]{2,1,0:T(8,128)(2,1)S(1)} collective-permute-done((bf16[2,384,384]{2,1,0:T(8,128)(2,1)S(1)}, bf16[2,384,384]{2,1,0:T(8,128)(2,1)S(1)}, u32[]{:S(2)}, u32[]{:S(2)}) %collective-permute-start.7) | collective-permute-done | bytes 589856 | tf_op jit(solution)/shard_map/ppermute | solution.py:308
  48.6 3.2 %shard_map.32 = bf16[2,384,384]{2,1,0:T(8,128)(2,1)} custom-call(bf16[2,384,384]{2,1,0:T(8,128)(2,1)S(1)} %get-tuple-element.7.own, bf16[2,384,384]{2,1,0:T(8,128)(2,1)S(1)} %shard_map.31.mine, bf16[2,384,384]{2,1,0:T(8,128)(2,1)S(1)} %collective-permute-done.7.other, bf16[3,384,384]{2,1,0:T(8,128)(2,1)S(1)} %get-tuple-element.8.weights), custom_call_target="tpu_custom_call" | custom-call | tf_op jit(solution)/shard_map/pallas_call | solution.py:291
Async XLA Ops:
  0.0 2.8 %collective-permute-start = (bf16[2,384,384]{2,1,0:T(8,128)(2,1)}, bf16[2,384,384]{2,1,0:T(8,128)(2,1)S(1)}, u32[]{:S(2)}, u32[]{:S(2)}) collective-permute-start(bf16[2,384,384]{2,1,0:T(8,128)(2,1)} %bitcast.4), channel_id=1, source_target_pairs={{0,1},{1,0},{2,3},{3,2},{4,5},{5,4},{6,7},{7,6},{8,9},{9,8},{10,11... | collective-permute-start | bytes 1769480 | tf_op jit(solution)/shard_map/ppermute | solution.py:308
  2.0 3.4 %collective-permute-start.3 = (bf16[2,384,384]{2,1,0:T(8,128)(2,1)S(1)}, bf16[2,384,384]{2,1,0:T(8,128)(2,1)S(1)}, u32[]{:S(2)}, u32[]{:S(2)}) collective-permute-start(bf16[2,384,384]{2,1,0:T(8,128)(2,1)S(1)} %get-tuple-element.7.own), channel_id=1, source_target_pairs={{0,2},{2,0},{28,30},{30,28},{1,3},{3,1},{29,31},{31,29}} | collective-permute-start | bytes 1769480 | tf_op jit(solution)/shard_map/ppermute | solution.py:305
  2.8 20.7 %collective-permute-start.2 = (bf16[2,384,384]{2,1,0:T(8,128)(2,1)S(1)}, bf16[2,384,384]{2,1,0:T(8,128)(2,1)S(1)}, u32[]{:S(2)}, u32[]{:S(2)}) collective-permute-start(bf16[2,384,384]{2,1,0:T(8,128)(2,1)S(1)} %shard_map.28), channel_id=1, source_target_pairs={{28,14},{30,16},{6,22},{24,8},{29,15},{31,17},{7,23},{25,9}} | collective-permute-start | bytes 1769480 | tf_op jit(solution)/shard_map/ppermute | solution.py:305
  4.1 19.4 %collective-permute-start.1 = (bf16[2,384,384]{2,1,0:T(8,128)(2,1)S(1)}, bf16[2,384,384]{2,1,0:T(8,128)(2,1)S(1)}, u32[]{:S(2)}, u32[]{:S(2)}) collective-permute-start(bf16[2,384,384]{2,1,0:T(8,128)(2,1)S(1)} %shard_map.28), channel_id=1, source_target_pairs={{0,14},{2,16},{4,18},{8,22},{22,8},{26,12},{1,15},{3,17},{5,19},{9... | collective-permute-start | bytes 1769480 | tf_op jit(solution)/shard_map/ppermute | solution.py:305
  5.5 29.8 %collective-permute-start.6 = (bf16[2,384,384]{2,1,0:T(8,128)(2,1)S(1)}, bf16[2,384,384]{2,1,0:T(8,128)(2,1)S(1)}, u32[]{:S(2)}, u32[]{:S(2)}) collective-permute-start(bf16[2,384,384]{2,1,0:T(8,128)(2,1)S(1)} %collective-permute-done.3.ends), channel_id=1, source_target_pairs={{28,16},{30,14},{29,17},{31,15}} | collective-permute-start | bytes 1769480 | tf_op jit(solution)/shard_map/ppermute | solution.py:305
  24.8 13.0 %collective-permute-start.5 = (bf16[2,384,384]{2,1,0:T(8,128)(2,1)S(1)}, bf16[2,384,384]{2,1,0:T(8,128)(2,1)S(1)}, u32[]{:S(2)}, u32[]{:S(2)}) collective-permute-start(bf16[2,384,384]{2,1,0:T(8,128)(2,1)S(1)} %shard_map.29), channel_id=1, source_target_pairs={{14,28},{16,30},{15,29},{17,31}} | collective-permute-start | bytes 1769480 | tf_op jit(solution)/shard_map/ppermute | solution.py:305
  26.2 16.4 %collective-permute-start.4 = (bf16[2,384,384]{2,1,0:T(8,128)(2,1)S(1)}, bf16[2,384,384]{2,1,0:T(8,128)(2,1)S(1)}, u32[]{:S(2)}, u32[]{:S(2)}) collective-permute-start(bf16[2,384,384]{2,1,0:T(8,128)(2,1)S(1)} %shard_map.29), channel_id=1, source_target_pairs={{14,0},{16,2},{0,16},{2,14},{18,4},{22,20},{20,6},{10,24},{8,10},{... | collective-permute-start | bytes 1769480 | tf_op jit(solution)/shard_map/ppermute | solution.py:305
  44.8 3.8 %collective-permute-start.7 = (bf16[2,384,384]{2,1,0:T(8,128)(2,1)S(1)}, bf16[2,384,384]{2,1,0:T(8,128)(2,1)S(1)}, u32[]{:S(2)}, u32[]{:S(2)}) collective-permute-start(bf16[2,384,384]{2,1,0:T(8,128)(2,1)S(1)} %shard_map.31.mine), channel_id=1, source_target_pairs={{0,1},{1,0},{2,3},{3,2},{4,5},{5,4},{6,7},{7,6},{8,9},{9,8},{10,11... | collective-permute-start | bytes 1769480 | tf_op jit(solution)/shard_map/ppermute | solution.py:308

commit v3 on v2

--- a/solution.py
+++ b/solution.py
@@ -102,9 +102,10 @@
         "first": inward[:2],
         "other": inward[2:],
         "ends": [(low0, low1), (low1, low0), (high0, high1), (high1, high0)],
-        "second": [(mid0, low0), (mid1, low1), (low0, mid1), (low1, mid0)],
+        "second": [(mid0, low0), (mid1, low1)],
         "third": [(mid0, high0), (mid1, high1)],
-        "inner": [(high0, mid1), (high1, mid0)],
+        "below": [(low0, mid1), (low1, mid0)],
+        "above": [(high0, mid1), (high1, mid0)],
     }
     busy = {link for flow in inward for link in links(*flow)}
     taken = {link for flow in plan["ends"] for link in links(*flow)}
@@ -130,6 +131,7 @@
             return None
     plan["lows"], plan["mids"], plan["highs"] = ([a, b] for a, b in zip(*threes))
     plan["direct"] = direct
+    plan["senders"] = [source for source, _ in plan["first"][2:] + plan["other"][2:]]
     plan["relayed"] = [relay for relay, _ in relays]
     plan["late"] = [source for source, _ in late]
     plan["second_pairs"] = [target for _, target in late + relays]
@@ -207,31 +209,29 @@
         copy.wait()
 
 
-def loaded(*blocks):
-    return pl.pallas_call(
-        load_kernel,
-        out_shape=[jax.ShapeDtypeStruct(block.shape, block.dtype) for block in blocks],
-        in_specs=[pl.BlockSpec(memory_space=pltpu.HBM)] * len(blocks),
-        out_specs=[pl.BlockSpec(memory_space=pltpu.VMEM)] * len(blocks),
-        scratch_shapes=[pltpu.SemaphoreType.DMA((len(blocks),))],
-        compiler_params=pltpu.CompilerParams(vmem_limit_bytes=VMEM_LIMIT),
-        name="load_kernel",
-    )(*(pltpu.with_memory_space_constraint(block, pltpu.HBM) for block in blocks))
-
-
-def first_kernel(plan, own, beside, weights, send):
+def first_kernel(plan, own, beside, weights, send, held, sems):
     size = own.shape[-1]
-    is_end = among(plan["lows"] + plan["highs"])
-
-    @pl.when(is_end)
-    def _():
-        sigma = self_energy(own, beside, weights)
+
+    @pl.when(among(plan["lows"] + plan["highs"]))
+    def _():
+        blocks, rows = held
+        copies = [
+            pltpu.make_async_copy(own, blocks, sems.at[0]),
+            pltpu.make_async_copy(weights, rows, sems.at[1]),
+        ]
+        for copy in copies:
+            copy.start()
+        for copy in copies:
+            copy.wait()
+        sigma = self_energy(blocks, beside, rows)
         send[0] = sigma[:size]
         send[1] = sigma[size:]
 
-    @pl.when(jnp.logical_not(is_end))
-    def _():
-        send[...] = own[...]
+    @pl.when(among(plan["senders"]))
+    def _():
+        copy = pltpu.make_async_copy(own, send, sems.at[0])
+        copy.start()
+        copy.wait()
 
 
 def sigma_kernel(plan, own, beside, weights, sigma_out):
@@ -244,36 +244,38 @@
         sigma_out[1] = sigma[size:]
 
 
-def second_kernel(plan, own, first, other, ends, send):
+def second_kernel(plan, own, first, other, send):
     @pl.when(among(plan["mids"]))
     def _():
         sigma = [added(first[part], other[part]) for part in range(2)]
         put(send, stepped(own, *sigma))
 
-    for members, source in (
-        (plan["relayed"], other),
-        (plan["late"], own),
-        (plan["lows"], ends),
-    ):
+    for members, source in ((plan["relayed"], other), (plan["late"], own)):
 
         @pl.when(among(members))
         def _():
             send[...] = source[...]
 
 
-def neighbour_kernel(plan, first, second, third, inner, sigma, out):
+def middle_kernel(plan, below, above, sigma, out):
     @pl.when(among(plan["mids"]))
     def _():
-        steps = [stepped(block, sigma[0], sigma[1]) for block in (second, inner)]
+        steps = [stepped(block, sigma[0], sigma[1]) for block in (below, above)]
         put(out, [added(*(step[part].astype(out.dtype) for step in steps)) for part in range(2)])
 
+
+def neighbour_kernel(plan, first, second, third, middle, sigma, out):
     for members, source in ((plan["direct"], first), (plan["second_pairs"], second)):
 
         @pl.when(among(members))
         def _():
             put(out, stepped(source, sigma[0], sigma[1]))
 
-    for members, source in ((plan["lows"], second), (plan["highs"], third)):
+    for members, source in (
+        (plan["lows"], second),
+        (plan["mids"], middle),
+        (plan["highs"], third),
+    ):
 
         @pl.when(among(members))
         def _():
@@ -286,37 +288,79 @@
     put(out, stepped(own, sigma[:size], sigma[size:]))
 
 
+LIMITS = pltpu.CompilerParams(vmem_limit_bytes=VMEM_LIMIT)
+IN_VMEM = pl.BlockSpec(memory_space=pltpu.VMEM)
+IN_HBM = pl.BlockSpec(memory_space=pltpu.HBM)
+
+
+def like(block, space=jax.ShapeDtypeStruct):
+    return space(block.shape, block.dtype)
+
+
 def call(kernel, plan, *blocks):
-    space = pl.BlockSpec(memory_space=pltpu.VMEM)
     return pl.pallas_call(
         functools.partial(kernel, plan),
-        out_shape=jax.ShapeDtypeStruct(blocks[0].shape, blocks[0].dtype),
-        in_specs=[space] * len(blocks),
-        out_specs=space,
-        compiler_params=pltpu.CompilerParams(vmem_limit_bytes=VMEM_LIMIT),
+        out_shape=like(blocks[0]),
+        in_specs=[IN_VMEM] * len(blocks),
+        out_specs=IN_VMEM,
+        compiler_params=LIMITS,
     )(*blocks)
 
 
+def loaded(own, weights):
+    return pl.pallas_call(
+        load_kernel,
+        out_shape=[like(own), like(weights)],
+        in_specs=[IN_HBM] * 2,
+        out_specs=[IN_VMEM] * 2,
+        scratch_shapes=[pltpu.SemaphoreType.DMA((2,))],
+        compiler_params=LIMITS,
+        name="load_kernel",
+    )(own, weights)
+
+
+def first_sent(plan, own, beside, weights):
+    return pl.pallas_call(
+        functools.partial(first_kernel, plan),
+        out_shape=like(own),
+        in_specs=[IN_HBM, IN_VMEM, IN_HBM],
+        out_specs=IN_VMEM,
+        scratch_shapes=[
+            (like(own, pltpu.VMEM), like(weights, pltpu.VMEM)),
+            pltpu.SemaphoreType.DMA((2,)),
+        ],
+        compiler_params=LIMITS,
+        name="first_kernel",
+    )(own, beside, weights)
+
+
 def chained(plan, green0, coupling):
-    own, weights = green0[0, 0], coupling[0]
     slabs = lax.axis_size("slab")
+    everyone = range(lax.axis_size("energy"))
+    outer = plan["lows"] + plan["highs"]
 
     def sent(value, flows):
         return lax.ppermute(value, "energy", plan[flows])
 
-    def swapped(value):
-        return lax.ppermute(value, "slab", [(s, slabs - 1 - s) for s in range(slabs)])
-
-    beside = swapped(own)
-    own, weights = loaded(own, weights)
-    send = call(first_kernel, plan, own, beside, weights)
-    ends, other, first = sent(own, "ends"), sent(send, "other"), sent(send, "first")
-    inner = sent(ends, "inner")
+    def swapped(value, members):
+        flows = [(e * slabs + s, e * slabs + slabs - 1 - s) for e in members for s in range(slabs)]
+        return lax.ppermute(value, ("energy", "slab"), flows)
+
+    far = pltpu.with_memory_space_constraint(green0[0, 0], pltpu.HBM)
+    far_weights = pltpu.with_memory_space_constraint(coupling[0], pltpu.HBM)
+    beside = swapped(green0[0, 0], outer)
+    ends = sent(green0[0, 0], "ends")
+    send = first_sent(plan, far, beside, far_weights)
+    other, first = sent(send, "other"), sent(send, "first")
+    own, weights = loaded(far, far_weights)
+    beside = swapped(own, [e for e in everyone if e not in outer])
+    above, below = sent(ends, "above"), sent(ends, "below")
     sigma = call(sigma_kernel, plan, own, beside, weights)
-    send = call(second_kernel, plan, own, first, other, ends)
+    send = call(second_kernel, plan, own, first, other)
     second, third = sent(send, "second"), sent(send, "third")
-    green = call(neighbour_kernel, plan, first, second, third, inner, sigma)
-    out = call(last_kernel, plan, own, green, swapped(green), weights)
+    middle = call(middle_kernel, plan, below, above, sigma)
+    green = call(neighbour_kernel, plan, first, second, third, middle, sigma)
+    out = call(last_kernel, plan, own, green, swapped(green, everyone), weights)
     return out[None, None]
 
 

time: 52.1 us -> 52.6 us (level)
  the two profiles are of different devices: /device:TPU:15 before, /device:TPU:0 now
where the time goes in v3:
time: 52.6 us; the launch traced here: 52.3 us
  waiting for transfers between devices  31.2 us (59%)
  starting transfers between devices  13.6 us (26%)
  Pallas kernels  7.45 us (14%)
    ppermute x7, waiting for transfers between devices, sent(): return lax.ppermute(value, 'energy', plan[flows])  29.2 us
    ppermute x7, starting transfers between devices, sent(): return lax.ppermute(value, 'energy', plan[flows])  10.4 us
    pallas_call x5, Pallas kernels, call(): pl.pallas_call(functools.partial(kernel, plan), out_shape=like(blocks[0])...  3.32 us
    ppermute x3, starting transfers between devices, swapped(): return lax.ppermute(value, ('energy', 'slab'), flows)  3.16 us
    pallas_call x1, Pallas kernels, first_sent(): pl.pallas_call(functools.partial(first_kernel, plan), out_shape=like(own)...  2.76 us
    ppermute x3, waiting for transfers between devices, swapped(): return lax.ppermute(value, ('energy', 'slab'), flows)  2 us
    pallas_call x1, Pallas kernels, loaded(): pl.pallas_call(load_kernel, out_shape=[like(own), like(weights)], in_spec...  1.37 us
  transfers between devices with their start and end apart: 10, of which 5 were waited for; matrix products, arithmetic and copies ran while one was open for 0% of the time, Pallas kernels for 8%

profile of v3, /device:TPU:0, one launch (start us, length us, event | category | flops | bytes accessed | tf_op | source)
XLA Modules:
  0.0 52.3 jit_solution(9041753015573738598)
XLA Ops:
  0.0 2.4 %collective-permute-start = (bf16[2,384,384]{2,1,0:T(8,128)(2,1)}, bf16[2,384,384]{2,1,0:T(8,128)(2,1)S(1)}, u32[]{:S(2)}, u32[]{:S(2)}) collective-permute-start(bf16[2,384,384]{2,1,0:T(8,128)(2,1)} %bitcast.5), channel_id=1, source_target_pairs={{0,1},{1,0},{2,3},{3,2},{28,29},{29,28},{30,31},{31,30}} | collective-permute-start | bytes 1769480 | tf_op jit(solution)/shard_map/ppermute | solution.py:347
  2.4 4.4 %collective-permute-start.5 = (bf16[2,384,384]{2,1,0:T(8,128)(2,1)}, bf16[2,384,384]{2,1,0:T(8,128)(2,1)S(1)}, u32[]{:S(2)}, u32[]{:S(2)}) collective-permute-start(bf16[2,384,384]{2,1,0:T(8,128)(2,1)} %bitcast.6), channel_id=1, source_target_pairs={{0,2},{2,0},{28,30},{30,28},{1,3},{3,1},{29,31},{31,29}} | collective-permute-start | bytes 1769480 | tf_op jit(solution)/shard_map/ppermute | solution.py:343
  6.8 0.0 collective-permute-done.beside
  6.8 2.8 %first_kernel.1 = bf16[2,384,384]{2,1,0:T(8,128)(2,1)S(1)} custom-call(bf16[2,384,384]{2,1,0:T(8,128)(2,1)} %bitcast.7, bf16[2,384,384]{2,1,0:T(8,128)(2,1)S(1)} %collective-permute-done.beside, bf16[3,384,384]{2,1,0:T(8,128)(2,1)} %bitcast.3), custom_call_target="tpu_custom_call" | custom-call | tf_op jit(solution)/shard_map/first_kernel/pallas_call | solution.py:323
  9.6 1.3 %collective-permute-start.1 = (bf16[2,384,384]{2,1,0:T(8,128)(2,1)S(1)}, bf16[2,384,384]{2,1,0:T(8,128)(2,1)S(1)}, u32[]{:S(2)}, u32[]{:S(2)}) collective-permute-start(bf16[2,384,384]{2,1,0:T(8,128)(2,1)S(1)} %first_kernel.1), channel_id=1, source_target_pairs={{0,14},{2,16},{4,18},{8,22},{22,8},{26,12},{1,15},{3,17},{5,19},{9... | collective-permute-start | bytes 1769480 | tf_op jit(solution)/shard_map/ppermute | solution.py:343
  10.9 0.7 %collective-permute-start.2 = (bf16[2,384,384]{2,1,0:T(8,128)(2,1)S(1)}, bf16[2,384,384]{2,1,0:T(8,128)(2,1)S(1)}, u32[]{:S(2)}, u32[]{:S(2)}) collective-permute-start(bf16[2,384,384]{2,1,0:T(8,128)(2,1)S(1)} %first_kernel.1), channel_id=1, source_target_pairs={{28,14},{30,16},{6,22},{24,8},{29,15},{31,17},{7,23},{25,9}} | collective-permute-start | bytes 1769480 | tf_op jit(solution)/shard_map/ppermute | solution.py:343
  11.6 1.4 %load_kernel.1 = (bf16[2,384,384]{2,1,0:T(8,128)(2,1)S(1)}, bf16[3,384,384]{2,1,0:T(8,128)(2,1)S(1)}) custom-call(bf16[2,384,384]{2,1,0:T(8,128)(2,1)} %bitcast.8, bf16[3,384,384]{2,1,0:T(8,128)(2,1)} %bitcast.4), custom_call_target="tpu_custom_call" | custom-call | tf_op jit(solution)/shard_map/load_kernel/pallas_call | solution.py:311
  13.0 0.7 %collective-permute-start.8 = (bf16[2,384,384]{2,1,0:T(8,128)(2,1)S(1)}, bf16[2,384,384]{2,1,0:T(8,128)(2,1)S(1)}, u32[]{:S(2)}, u32[]{:S(2)}) collective-permute-start(bf16[2,384,384]{2,1,0:T(8,128)(2,1)S(1)} %get-tuple-element.7.own), channel_id=1, source_target_pairs={{4,5},{5,4},{6,7},{7,6},{8,9},{9,8},{10,11},{11,10},{12,13},{13,12... | collective-permute-start | bytes 1769480 | tf_op jit(solution)/shard_map/ppermute | solution.py:347
  13.7 7.3 %collective-permute-done.5 = bf16[2,384,384]{2,1,0:T(8,128)(2,1)S(1)} collective-permute-done((bf16[2,384,384]{2,1,0:T(8,128)(2,1)}, bf16[2,384,384]{2,1,0:T(8,128)(2,1)S(1)}, u32[]{:S(2)}, u32[]{:S(2)}) %collective-permute-start.5) | collective-permute-done | bytes 589856 | tf_op jit(solution)/shard_map/ppermute | solution.py:343
  21.0 1.3 %collective-permute-start.6 = (bf16[2,384,384]{2,1,0:T(8,128)(2,1)S(1)}, bf16[2,384,384]{2,1,0:T(8,128)(2,1)S(1)}, u32[]{:S(2)}, u32[]{:S(2)}) collective-permute-start(bf16[2,384,384]{2,1,0:T(8,128)(2,1)S(1)} %collective-permute-done.5), channel_id=1, source_target_pairs={{0,16},{2,14},{1,17},{3,15}} | collective-permute-start | bytes 1769480 | tf_op jit(solution)/shard_map/ppermute | solution.py:343
  22.3 0.7 %collective-permute-start.7 = (bf16[2,384,384]{2,1,0:T(8,128)(2,1)S(1)}, bf16[2,384,384]{2,1,0:T(8,128)(2,1)S(1)}, u32[]{:S(2)}, u32[]{:S(2)}) collective-permute-start(bf16[2,384,384]{2,1,0:T(8,128)(2,1)S(1)} %collective-permute-done.5), channel_id=1, source_target_pairs={{28,16},{30,14},{29,17},{31,15}} | collective-permute-start | bytes 1769480 | tf_op jit(solution)/shard_map/ppermute | solution.py:343
  23.0 1.6 %collective-permute-done.1.first = bf16[2,384,384]{2,1,0:T(8,128)(2,1)S(1)} collective-permute-done((bf16[2,384,384]{2,1,0:T(8,128)(2,1)S(1)}, bf16[2,384,384]{2,1,0:T(8,128)(2,1)S(1)}, u32[]{:S(2)}, u32[]{:S(2)}) %collective-permute-start.1) | collective-permute-done | bytes 589856 | tf_op jit(solution)/shard_map/ppermute | solution.py:343
  24.6 0.0 collective-permute-done.2.other
  24.6 1.3 %collective-permute-start.3 = (bf16[2,384,384]{2,1,0:T(8,128)(2,1)S(1)}, bf16[2,384,384]{2,1,0:T(8,128)(2,1)S(1)}, u32[]{:S(2)}, u32[]{:S(2)}) collective-permute-start(bf16[2,384,384]{2,1,0:T(8,128)(2,1)S(1)} %shard_map.28), channel_id=1, source_target_pairs={{14,0},{16,2},{18,4},{22,20},{20,6},{10,24},{8,10},{12,26},{15,1},... | collective-permute-start | bytes 1769480 | tf_op jit(solution)/shard_map/ppermute | solution.py:343
  25.9 0.7 %collective-permute-start.4 = (bf16[2,384,384]{2,1,0:T(8,128)(2,1)S(1)}, bf16[2,384,384]{2,1,0:T(8,128)(2,1)S(1)}, u32[]{:S(2)}, u32[]{:S(2)}) collective-permute-start(bf16[2,384,384]{2,1,0:T(8,128)(2,1)S(1)} %shard_map.28), channel_id=1, source_target_pairs={{14,28},{16,30},{15,29},{17,31}} | collective-permute-start | bytes 1769480 | tf_op jit(solution)/shard_map/ppermute | solution.py:343
  26.6 0.0 collective-permute-done.8.beside
  26.6 10.1 %collective-permute-done.6.below = bf16[2,384,384]{2,1,0:T(8,128)(2,1)S(1)} collective-permute-done((bf16[2,384,384]{2,1,0:T(8,128)(2,1)S(1)}, bf16[2,384,384]{2,1,0:T(8,128)(2,1)S(1)}, u32[]{:S(2)}, u32[]{:S(2)}) %collective-permute-start.6) | collective-permute-done | bytes 589856 | tf_op jit(solution)/shard_map/ppermute | solution.py:343
  36.8 0.0 collective-permute-done.7.above
  36.8 10.2 %collective-permute-done.3.second = bf16[2,384,384]{2,1,0:T(8,128)(2,1)S(1)} collective-permute-done((bf16[2,384,384]{2,1,0:T(8,128)(2,1)S(1)}, bf16[2,384,384]{2,1,0:T(8,128)(2,1)S(1)}, u32[]{:S(2)}, u32[]{:S(2)}) %collective-permute-start.3) | collective-permute-done | bytes 589856 | tf_op jit(solution)/shard_map/ppermute | solution.py:343
  47.0 0.0 collective-permute-done.4.third
  47.0 0.1 shard_map.31.mine
  47.0 0.1 collective-permute-start.9
  47.1 2.0 %collective-permute-done.9.other = bf16[2,384,384]{2,1,0:T(8,128)(2,1)S(1)} collective-permute-done((bf16[2,384,384]{2,1,0:T(8,128)(2,1)S(1)}, bf16[2,384,384]{2,1,0:T(8,128)(2,1)S(1)}, u32[]{:S(2)}, u32[]{:S(2)}) %collective-permute-start.9) | collective-permute-done | bytes 589856 | tf_op jit(solution)/shard_map/ppermute | solution.py:347
  49.1 3.2 %shard_map.32 = bf16[2,384,384]{2,1,0:T(8,128)(2,1)} custom-call(bf16[2,384,384]{2,1,0:T(8,128)(2,1)S(1)} %get-tuple-element.7.own, bf16[2,384,384]{2,1,0:T(8,128)(2,1)S(1)} %shard_map.31.mine, bf16[2,384,384]{2,1,0:T(8,128)(2,1)S(1)} %collective-permute-done.9.other, bf16[3,384,384]{2,1,0:T(8,128)(2,1)S(1)} %get-tuple-element.8.weights), custom_call_target="tpu_custom_call" | custom-call | tf_op jit(solution)/shard_map/pallas_call | solution.py:301
  (3 shorter events, 0.0 us)
Async XLA Ops:
  0.0 6.8 %collective-permute-start = (bf16[2,384,384]{2,1,0:T(8,128)(2,1)}, bf16[2,384,384]{2,1,0:T(8,128)(2,1)S(1)}, u32[]{:S(2)}, u32[]{:S(2)}) collective-permute-start(bf16[2,384,384]{2,1,0:T(8,128)(2,1)} %bitcast.5), channel_id=1, source_target_pairs={{0,1},{1,0},{2,3},{3,2},{28,29},{29,28},{30,31},{31,30}} | collective-permute-start | bytes 1769480 | tf_op jit(solution)/shard_map/ppermute | solution.py:347
  2.4 18.6 %collective-permute-start.5 = (bf16[2,384,384]{2,1,0:T(8,128)(2,1)}, bf16[2,384,384]{2,1,0:T(8,128)(2,1)S(1)}, u32[]{:S(2)}, u32[]{:S(2)}) collective-permute-start(bf16[2,384,384]{2,1,0:T(8,128)(2,1)} %bitcast.6), channel_id=1, source_target_pairs={{0,2},{2,0},{28,30},{30,28},{1,3},{3,1},{29,31},{31,29}} | collective-permute-start | bytes 1769480 | tf_op jit(solution)/shard_map/ppermute | solution.py:343
  9.6 15.0 %collective-permute-start.1 = (bf16[2,384,384]{2,1,0:T(8,128)(2,1)S(1)}, bf16[2,384,384]{2,1,0:T(8,128)(2,1)S(1)}, u32[]{:S(2)}, u32[]{:S(2)}) collective-permute-start(bf16[2,384,384]{2,1,0:T(8,128)(2,1)S(1)} %first_kernel.1), channel_id=1, source_target_pairs={{0,14},{2,16},{4,18},{8,22},{22,8},{26,12},{1,15},{3,17},{5,19},{9... | collective-permute-start | bytes 1769480 | tf_op jit(solution)/shard_map/ppermute | solution.py:343
  10.9 13.7 %collective-permute-start.2 = (bf16[2,384,384]{2,1,0:T(8,128)(2,1)S(1)}, bf16[2,384,384]{2,1,0:T(8,128)(2,1)S(1)}, u32[]{:S(2)}, u32[]{:S(2)}) collective-permute-start(bf16[2,384,384]{2,1,0:T(8,128)(2,1)S(1)} %first_kernel.1), channel_id=1, source_target_pairs={{28,14},{30,16},{6,22},{24,8},{29,15},{31,17},{7,23},{25,9}} | collective-permute-start | bytes 1769480 | tf_op jit(solution)/shard_map/ppermute | solution.py:343
  13.0 13.6 %collective-permute-start.8 = (bf16[2,384,384]{2,1,0:T(8,128)(2,1)S(1)}, bf16[2,384,384]{2,1,0:T(8,128)(2,1)S(1)}, u32[]{:S(2)}, u32[]{:S(2)}) collective-permute-start(bf16[2,384,384]{2,1,0:T(8,128)(2,1)S(1)} %get-tuple-element.7.own), channel_id=1, source_target_pairs={{4,5},{5,4},{6,7},{7,6},{8,9},{9,8},{10,11},{11,10},{12,13},{13,12... | collective-permute-start | bytes 1769480 | tf_op jit(solution)/shard_map/ppermute | solution.py:347
  21.0 15.8 %collective-permute-start.6 = (bf16[2,384,384]{2,1,0:T(8,128)(2,1)S(1)}, bf16[2,384,384]{2,1,0:T(8,128)(2,1)S(1)}, u32[]{:S(2)}, u32[]{:S(2)}) collective-permute-start(bf16[2,384,384]{2,1,0:T(8,128)(2,1)S(1)} %collective-permute-done.5), channel_id=1, source_target_pairs={{0,16},{2,14},{1,17},{3,15}} | collective-permute-start | bytes 1769480 | tf_op jit(solution)/shard_map/ppermute | solution.py:343
  22.3 14.4 %collective-permute-start.7 = (bf16[2,384,384]{2,1,0:T(8,128)(2,1)S(1)}, bf16[2,384,384]{2,1,0:T(8,128)(2,1)S(1)}, u32[]{:S(2)}, u32[]{:S(2)}) collective-permute-start(bf16[2,384,384]{2,1,0:T(8,128)(2,1)S(1)} %collective-permute-done.5), channel_id=1, source_target_pairs={{28,16},{30,14},{29,17},{31,15}} | collective-permute-start | bytes 1769480 | tf_op jit(solution)/shard_map/ppermute | solution.py:343
  24.6 22.4 %collective-permute-start.3 = (bf16[2,384,384]{2,1,0:T(8,128)(2,1)S(1)}, bf16[2,384,384]{2,1,0:T(8,128)(2,1)S(1)}, u32[]{:S(2)}, u32[]{:S(2)}) collective-permute-start(bf16[2,384,384]{2,1,0:T(8,128)(2,1)S(1)} %shard_map.28), channel_id=1, source_target_pairs={{14,0},{16,2},{18,4},{22,20},{20,6},{10,24},{8,10},{12,26},{15,1},... | collective-permute-start | bytes 1769480 | tf_op jit(solution)/shard_map/ppermute | solution.py:343
  25.9 21.1 %collective-permute-start.4 = (bf16[2,384,384]{2,1,0:T(8,128)(2,1)S(1)}, bf16[2,384,384]{2,1,0:T(8,128)(2,1)S(1)}, u32[]{:S(2)}, u32[]{:S(2)}) collective-permute-start(bf16[2,384,384]{2,1,0:T(8,128)(2,1)S(1)} %shard_map.28), channel_id=1, source_target_pairs={{14,28},{16,30},{15,29},{17,31}} | collective-permute-start | bytes 1769480 | tf_op jit(solution)/shard_map/ppermute | solution.py:343
  47.0 2.1 %collective-permute-start.9 = (bf16[2,384,384]{2,1,0:T(8,128)(2,1)S(1)}, bf16[2,384,384]{2,1,0:T(8,128)(2,1)S(1)}, u32[]{:S(2)}, u32[]{:S(2)}) collective-permute-start(bf16[2,384,384]{2,1,0:T(8,128)(2,1)S(1)} %shard_map.31.mine), channel_id=1, source_target_pairs={{0,1},{1,0},{2,3},{3,2},{4,5},{5,4},{6,7},{7,6},{8,9},{9,8},{10,11... | collective-permute-start | bytes 1769480 | tf_op jit(solution)/shard_map/ppermute | solution.py:347
